TPU v7x, 512 devices: a whole 4x4x16 slice. The times are simulated.
512 devices in a mesh: row: 32 (over x, z_lo), col: 16 (over y, z_hi, core).
Axes of the slice: x: 4, y: 4, z: 16 (z_hi: 2, z_lo: 8; z = z_hi * 8 + z_lo), core: 2. Of those that a mesh axis runs over, the one named last changes fastest.
Arguments:
- ancestor: float32 [12288, 12288], P('row', 'col'), may hold values from -6 to 6
- pattern: int32 [96, 96], P('row', 'col'), may hold values 0 or 1
- member: int32 [96, 2], replicated, may hold values 0 or 1
- panel: float32 [12288, 512], P('col', 'row'), may hold values from -0.0546875 to 0.0546875
- diag_inv: float32 [256, 512], P(None, 'col'), may hold values from -6 to 6
Outputs:
- ancestor_panel: float32 [12288, 512], P('row', 'col')
- diag_blocks: float32 [256, 512], P(None, 'col')
All inputs are finite; a program needn't handle non-finite values. No bound on the sum of `pattern` on one device may be relied on, other than what follows from the above.
Results may differ from a plain program's by a relative error of at most 0.0001.
Values sent between devices are 32-bit elements; how exact they have to be, the bound alone decides.
No kernel may reach another device: no remote copies, remote signals or barrier semaphores. Data moves between devices by JAX's collectives and lax.ppermute only.
A program may use at most 64 MiB of HBM per device.

v0:
```python
import jax
import jax.numpy as jnp
from jax import lax
from jax.sharding import PartitionSpec as P

W = 256
BS = 128


def spread(block, axis, owner):
    block = jnp.where(lax.axis_index(axis) == owner, block, jnp.zeros_like(block))
    return lax.psum(block, axis)


def pick_member(member, start, count, which):
    rows = lax.dynamic_slice_in_dim(member, start, count, 0).astype(jnp.float32)
    return jnp.where(which == 0, rows[:, 0], rows[:, 1])


def both_terms(normed_rows, values):
    first_term = jnp.dot(
        normed_rows[:, :W].T,
        values[:, :W],
        precision=lax.Precision.HIGHEST,
        preferred_element_type=jnp.float32,
    )
    second_term = jnp.dot(
        normed_rows[:, W:].T,
        values[:, W:],
        precision=lax.Precision.HIGHEST,
        preferred_element_type=jnp.float32,
    )
    return jnp.concatenate([first_term, second_term], axis=1)


def body(ancestor, pattern, member, panel, diag_inv):
    row_count = lax.axis_size("row")
    col_count = lax.axis_size("col")
    row_idx = lax.axis_index("row")
    col_idx = lax.axis_index("col")
    row_blocks, col_blocks = pattern.shape
    local_rows, local_cols = ancestor.shape
    slice_cols = panel.shape[1]
    panel_owner = row_idx * slice_cols // W
    chosen = pick_member(member, col_idx * col_blocks, col_blocks, panel_owner)
    masked_panel = (panel.reshape(col_blocks, BS, slice_cols) * chosen[:, None, None]).reshape(
        local_cols, slice_cols
    )
    full_cols = lax.all_gather(masked_panel, "row", axis=1, tiled=True)
    weights = pattern.astype(jnp.float32)
    masked = (ancestor.reshape(row_blocks, BS, col_blocks, BS) * weights[:, None, :, None]).reshape(
        local_rows, local_cols
    )
    partial_value = jnp.dot(
        masked, full_cols, precision=lax.Precision.HIGHEST, preferred_element_type=jnp.float32
    )
    own_cols = diag_inv.shape[1]
    own_owner = col_idx * own_cols // W
    picked = pick_member(member, row_idx * row_blocks, row_blocks, own_owner)
    keep_rows = jnp.repeat(picked, BS)
    fold_ratio = row_count // col_count
    sender = lax.dynamic_slice_in_dim(full_cols, row_idx % fold_ratio * local_rows, local_rows, 0)
    summed = lax.psum_scatter(partial_value, "col", scatter_dimension=1, tiled=True)
    ancestor_panel = -(summed * keep_rows[:, None])
    normed_rows = spread(sender, "col", row_idx // fold_ratio)
    block_term = both_terms(normed_rows, partial_value)
    totals = lax.psum(block_term, ("row", "col"))
    diag_out = diag_inv + lax.dynamic_slice_in_dim(totals, col_idx * own_cols, own_cols, 1)
    return (ancestor_panel, diag_out)


def solution(mesh):
    placed = (P("row", "col"), P("row", "col"), P(), P("col", "row"), P(None, "col"))
    return jax.shard_map(
        body,
        mesh=mesh,
        in_specs=placed,
        out_specs=(P("row", "col"), P(None, "col")),
        check_vma=False,
    )
```

profile of v0, /device:TPU:6, one launch (start us, length us, event | category | flops | bytes accessed | tf_op | source)
XLA Modules:
  0.0 1086.7 jit_solution(8966737498046524540)
XLA Ops:
  7.2 0.0 copy-start.4
  7.2 0.0 all-gather.2.cloned.1.call-start
  7.2 0.8 dynamic-slice_convert_fusion.1
  8.0 0.1 broadcast_bitcast_fusion
  8.1 1.4 broadcast_multiply_fusion
  9.5 0.0 all-gather.2.cloned.1.call-update
  9.5 0.0 all-reduce.3.cloned.1.call-start
  9.6 212.3 %all-gather.2.cloned.1.call-done = f32[768,512]{0,1:T(8,128)} async-done(((f32[768,16]{0,1:T(8,128)}), f32[768,512]{0,1:T(8,128)}) %all-gather.2.cloned.1.call-update) | async-done | bytes 1572880 | tf_op jit(solution)/shard_map/all_gather | solution.py:49
  221.9 2.2 dynamic-slice_select_fusion
  224.0 0.0 all-reduce.3.cloned.1.call-update
  224.0 0.0 all-reduce.5.cloned.1.call-start
  224.1 0.2 mul.50
  224.3 0.0 copy-done.1
  224.3 1.1 copy-done
  225.4 2.2 fusion
  227.6 274.0 %all-reduce.3.cloned.1.call-done = f32[384,512]{0,1:T(8,128)} async-done(((f32[384,512]{0,1:T(8,128)}), f32[384,512]{0,1:T(8,128)}) %all-reduce.3.cloned.1.call-update) | async-done | bytes 786448 | tf_op jit(solution)/shard_map/psum | solution.py:12
  501.7 1.8 fusion.2
  503.5 1.8 fusion.5
  505.3 0.8 pad_maximum_fusion
  506.1 0.0 all-reduce.5.cloned.1.call-update
  506.1 0.0 reduce-scatter.4.cloned.1.call-start
  506.2 1.2 copy.10
  507.3 0.0 reduce-scatter.4.cloned.1.call-update
  507.4 0.0 copy-done.3
  507.4 0.1 dynamic-slice_convert_fusion
  507.5 0.1 broadcast_bitcast_fusion.1
  507.6 466.2 %all-reduce.5.cloned.1.call-done = f32[256,512]{0,1:T(8,128)} async-done(((f32[256,512]{0,1:T(8,128)}), f32[256,512]{0,1:T(8,128)}) %all-reduce.5.cloned.1.call-update) | async-done | bytes 524304 | tf_op jit(solution)/shard_map/psum | solution.py:67
  973.7 1.4 dynamic-slice_add_fusion
  975.1 103.3 %reduce-scatter.4.cloned.1.call-done = f32[32,384]{1,0:T(8,128)} async-done(((f32[512,384]{1,0:T(8,128)}), f32[32,384]{1,0:T(8,128)}) %reduce-scatter.4.cloned.1.call-update) | async-done | bytes 49168
  1078.4 0.9 copy.11
  1079.3 0.1 multiply_negate_fusion
  1079.4 0.7 copy.9
  (9 shorter events, 0.0 us)
Async XLA Ops:
  7.2 216.9 %copy-start.4 = (s32[3,6]{1,0:T(4,128)S(1)}, s32[3,6]{1,0:T(4,128)}, u32[]{:S(2)}) copy-start(s32[3,6]{1,0:T(4,128)} %param.6) | copy-start | bytes 220
  7.2 214.7 %all-gather.2.cloned.1.call-start = ((), (), s32[]{:S(2)}) async-start(), calls=%async_computation.1 | async-start | bytes 1622016 | tf_op jit(solution)/shard_map/all_gather | solution.py:49
  9.5 492.1 %all-reduce.3.cloned.1.call-start = ((), (), s32[]{:S(2)}) async-start(), calls=%async_computation.2 | async-start | bytes 1572864 | tf_op jit(solution)/shard_map/psum | solution.py:12
  221.9 2.4 copy-start.1
  224.0 1.4 copy-start
  224.0 749.7 %all-reduce.5.cloned.1.call-start = ((), (), s32[]{:S(2)}) async-start(), calls=%async_computation.3 | async-start | bytes 1048576 | tf_op jit(solution)/shard_map/psum | solution.py:67
  506.1 1.3 copy-start.3
  506.1 467.6 %copy-start.2 = (f32[256,32]{0,1:T(8,128)S(1)}, f32[256,32]{0,1:T(8,128)}, u32[]{:S(2)}) copy-start(f32[256,32]{0,1:T(8,128)} %param.9) | copy-start | bytes 98308
  506.1 572.3 %reduce-scatter.4.cloned.1.call-start = ((), (), s32[]{:S(2)}) async-start(), calls=%async_computation.4 | async-start | bytes 835584
Sparse Core Ops, SparseCore 0:
  10.6 211.1 all-gather.1
  224.8 276.8 all-reduce.2
  507.1 466.5 all-reduce.4
  978.2 100.1 reduce-scatter.3
where the time goes:
time: 1090 us
  waiting for transfers between devices  1060 us (97%)
  between operations  13.9 us (1%)
    psum x1, waiting for transfers between devices, body(): totals = lax.psum(block_term, ('row', 'col'))  466 us
    psum x1, waiting for transfers between devices, spread(): return lax.psum(block, axis)  274 us
    all_gather x1, waiting for transfers between devices, body(): full_cols = lax.all_gather(masked_panel, 'row', axis=1, tiled=True)  212 us
    unnamed x5, waiting for transfers between devices  103 us
  transfers between devices with their start and end apart: 4, of which 4 were waited for; matrix products, arithmetic and copies ran while one was open for 0% of the time, Pallas kernels for 0%

commit v1 on v0

v1 whole, which is shorter than its diff:
```python
import jax
import jax.numpy as jnp
from jax import lax
from jax.sharding import Mesh, PartitionSpec as P

W = 256
BS = 128
ROW = ("x", "zl")
COL = ("y", "zh", "core")
SIZES = (4, 8, 4, 2, 2)
EXACT = lax.Precision.HIGH


def flat(x, zl, y, zh, core):
    return (((x * 8 + zl) * 4 + y) * 2 + zh) * 2 + core


def row_block_pairs():
    pairs = []
    for x in range(4):
        for zl in range(8):
            for y in range(4):
                for zh in range(2):
                    for core in range(2):
                        source = flat(y, zh * 4 + core * 2 + (zl & 1), x, zl >> 2, (zl >> 1) & 1)
                        pairs.append((source, flat(x, zl, y, zh, core)))
    return pairs


def ordered(bit, own, other, axis):
    low = jnp.where(bit == 0, own, other)
    high = jnp.where(bit == 0, other, own)
    return jnp.stack([low, high], axis=axis)


def xor_pairs(size, step):
    return [(i, i ^ step) for i in range(size)]


def keep_rows(member, start, count, which):
    rows = lax.dynamic_slice_in_dim(member, start, count, 0).astype(jnp.float32)
    return jnp.repeat(jnp.where(which == 0, rows[:, 0], rows[:, 1]), BS)


def body(ancestor, pattern, member, panel, diag_inv):
    x, zl = lax.axis_index("x"), lax.axis_index("zl")
    y, zh, core = lax.axis_index("y"), lax.axis_index("zh"), lax.axis_index("core")
    row, col = x * 8 + zl, (y * 2 + zh) * 2 + core
    row_blocks, col_blocks = pattern.shape
    rows, cols = ancestor.shape

    own = panel.T * keep_rows(member, col * col_blocks, col_blocks, x // 2)[None, :]
    part = ordered(zl // 4, own, lax.ppermute(own, "zl", xor_pairs(8, 4)), 0)
    part = ordered(zl // 2 % 2, part, lax.ppermute(part, "zl", xor_pairs(8, 2)), 0)
    part = ordered(zl % 2, part, lax.ppermute(part, "zl", xor_pairs(8, 1)), 2)
    part = part.reshape(128, cols)
    full = lax.all_to_all(jnp.broadcast_to(part[None], (4, 128, cols)), "x", 0, 0, tiled=True)

    half = lax.dynamic_slice(
        full.reshape(4, 2, 2, 32, cols),
        (x // 2 * 2, 0, 0, 0, zl % 2 * rows),
        (2, 2, 2, 32, rows),
    )
    normed_rows = lax.ppermute(
        half.transpose(0, 2, 1, 3, 4).reshape(W, rows), ROW + COL, row_block_pairs()
    )

    weights = pattern.astype(jnp.float32)
    masked = (
        ancestor.reshape(row_blocks, BS, col_blocks, BS) * weights[:, None, :, None]
    ).reshape(rows, cols)
    share = lax.dot_general(
        full.reshape(512, cols),
        masked,
        (((1,), (1,)), ((), ())),
        precision=EXACT,
        preferred_element_type=jnp.float32,
    )
    pieces = lax.all_to_all(share.reshape(8, 64, rows), ("y", "core"), 0, 0, tiled=True)
    summed = pieces.sum(0).reshape(2, 32, rows)
    mine = jnp.where(zh == 0, summed[0], summed[1])
    theirs = jnp.where(zh == 0, summed[1], summed[0])
    product = mine + lax.ppermute(theirs, "zh", xor_pairs(2, 1))
    kept = product * keep_rows(member, row * row_blocks, row_blocks, y // 2)[None, :]

    term = lax.dot_general(
        kept,
        normed_rows,
        (((1,), (1,)), ((), ())),
        precision=EXACT,
        preferred_element_type=jnp.float32,
    )
    owned = lax.all_to_all(term.reshape(32, 1, W), ROW, 0, 0, tiled=True).sum(0)
    total = lax.all_to_all(jnp.broadcast_to(owned[None], (32, 1, W)), ROW, 0, 0, tiled=True)
    diag_out = diag_inv + total.reshape(32, W).T
    return (-kept).T, diag_out


def solution(mesh):
    fine = Mesh(mesh.devices.reshape(SIZES), ROW + COL)
    placed = (P(ROW, COL), P(ROW, COL), P(), P(COL, ROW), P(None, COL))
    return jax.shard_map(
        body,
        mesh=fine,
        in_specs=placed,
        out_specs=(P(ROW, COL), P(None, COL)),
        check_vma=False,
    )
```

time: 1090 us -> 156 us (0.14)
  waiting for transfers between devices: 1060 us -> 49.1 us
  blocking collectives: 0 us -> 54.6 us
  starting transfers between devices: 0.16 us -> 41 us
  between operations: 13.9 us -> 0.86 us
    psum x2 -> x0, waiting for transfers between devices: 740 us -> none  [the longest x1 466 us: body(): totals = lax.psum(block_term, ('row', 'col'))]
    all_gather x1 -> x0, waiting for transfers between devices: 212 us -> none  [body(): full_cols = lax.all_gather(masked_panel, 'row', axis=1, tiled=True)]
    unnamed x5 -> x0, waiting for transfers between devices: 103 us -> none
    all_to_all x0 -> x2, blocking collectives: none -> 54.6 us  [the longest x1 38.9 us: body(): owned = lax.all_to_all(term.reshape(32, 1, W), ROW, 0, 0, tiled=True).sum(0)]
    ppermute x0 -> x5, starting transfers between devices: none -> 30.8 us  [the longest x1 9.09 us: body(): part = ordered(zl // 4, own, lax.ppermute(own, 'zl', xor_pairs(8, 4)), 0)]
    all_to_all x0 -> x2, waiting for transfers between devices: none -> 26.1 us  [the longest x1 16.5 us: body(): lax.all_to_all(jnp.broadcast_to(part[None], (4, 128, cols)), 'x', 0, 0, t...]
    ppermute x0 -> x5, waiting for transfers between devices: none -> 23 us  [the longest x1 10.9 us: body(): product = mine + lax.ppermute(theirs, 'zh', xor_pairs(2, 1))]
  transfers between devices with their start and end apart: 4 -> 7, of which waited for: 4 -> 6; matrix products, arithmetic and copies ran while one was open for 0% -> 1% of each run, Pallas kernels for 0% -> 0%
where the time goes in v1:
time: 156 us; the launch traced here: 154 us
  blocking collectives  54.6 us (35%)
  waiting for transfers between devices  49.1 us (31%)
  starting transfers between devices  41 us (26%)
  other arithmetic  3.92 us (3%)
  matrix products  2.67 us (2%)
  local copies, waits for them, and re-layouts  1.71 us (1%)
    all_to_all x1, blocking collectives, body(): owned = lax.all_to_all(term.reshape(32, 1, W), ROW, 0, 0, tiled=True).sum(0)  38.9 us
    all_to_all x1, waiting for transfers between devices, body(): lax.all_to_all(jnp.broadcast_to(part[None], (4, 128, cols)), 'x', 0, 0, t...  16.5 us
    all_to_all x1, blocking collectives, body(): lax.all_to_all(jnp.broadcast_to(owned[None], (32, 1, W)), ROW, 0, 0, tile...  15.8 us
    ppermute x1, waiting for transfers between devices, body(): product = mine + lax.ppermute(theirs, 'zh', xor_pairs(2, 1))  10.9 us
    all_to_all x1, waiting for transfers between devices, body(): lax.all_to_all(share.reshape(8, 64, rows), ('y', 'core'), 0, 0, tiled=True)  9.57 us
    ppermute x1, starting transfers between devices, body(): part = ordered(zl // 4, own, lax.ppermute(own, 'zl', xor_pairs(8, 4)), 0)  9.09 us
    ppermute x1, starting transfers between devices, body(): product = mine + lax.ppermute(theirs, 'zh', xor_pairs(2, 1))  7.12 us
    ppermute x1, starting transfers between devices, body(): lax.ppermute(half.transpose(0, 2, 1, 3, 4).reshape(W, rows), ROW + COL, r...  6.64 us
  transfers between devices with their start and end apart: 7, of which 6 were waited for; matrix products, arithmetic and copies ran while one was open for 1% of the time, Pallas kernels for 0%

profile of v1, /device:TPU:6, one launch (start us, length us, event | category | flops | bytes accessed | tf_op | source)
XLA Modules:
  0.0 153.9 jit_solution(3919620259339128297)
XLA Ops:
  0.7 0.8 dynamic-slice_convert_fusion.1
  1.4 0.1 broadcast_bitcast_fusion
  1.5 0.8 multiply_bitcast_fusion
  2.3 9.1 %collective-permute-start = (f32[16,768]{1,0:T(8,128)S(1)}, f32[16,768]{1,0:T(8,128)S(1)}, u32[]{:S(2)}, u32[]{:S(2)}) collective-permute-start(f32[16,768]{1,0:T(8,128)S(1)} %multiply_bitcast_fusion), channel_id=1, source_target_pairs={{0,64},{16,80},{32,96},{48,112},{64,0},{80,16},{96,32},{112,48},{1... | collective-permute-start | bytes 147464 | tf_op jit(solution)/shard_map/ppermute | solution.py:53
  11.4 2.0 %collective-permute-done = f32[16,768]{1,0:T(8,128)S(1)} collective-permute-done((f32[16,768]{1,0:T(8,128)S(1)}, f32[16,768]{1,0:T(8,128)S(1)}, u32[]{:S(2)}, u32[]{:S(2)}) %collective-permute-start) | collective-permute-done | bytes 49184 | tf_op jit(solution)/shard_map/ppermute | solution.py:53
  13.5 0.8 select_bitcast_fusion.5
  14.3 5.3 %collective-permute-start.1 = (f32[2,16,768]{2,1,0:T(8,128)S(1)}, f32[2,16,768]{2,1,0:T(8,128)S(1)}, u32[]{:S(2)}, u32[]{:S(2)}) collective-permute-start(f32[2,16,768]{2,1,0:T(8,128)S(1)} %pad_maximum_fusion.2), channel_id=1, source_target_pairs={{0,32},{16,48},{32,0},{48,16},{64,96},{80,112},{96,64},{112,80},{1... | collective-permute-start | bytes 294920 | tf_op jit(solution)/shard_map/ppermute | solution.py:54
  19.6 5.0 %collective-permute-done.1 = f32[2,16,768]{2,1,0:T(8,128)S(1)} collective-permute-done((f32[2,16,768]{2,1,0:T(8,128)S(1)}, f32[2,16,768]{2,1,0:T(8,128)S(1)}, u32[]{:S(2)}, u32[]{:S(2)}) %collective-permute-start.1) | collective-permute-done | bytes 98336 | tf_op jit(solution)/shard_map/ppermute | solution.py:54
  24.7 2.6 %collective-permute-start.2 = (f32[2,2,16,768]{3,2,1,0:T(8,128)S(1)}, f32[2,2,16,768]{3,2,1,0:T(8,128)S(1)}, u32[]{:S(2)}, u32[]{:S(2)}) collective-permute-start(f32[2,2,16,768]{3,2,1,0:T(8,128)S(1)} %pad_maximum_fusion.1), channel_id=1, source_target_pairs={{0,16},{16,0},{32,48},{48,32},{64,80},{80,64},{96,112},{112,96},{1... | collective-permute-start | bytes 589832 | tf_op jit(solution)/shard_map/ppermute | solution.py:55
  27.3 5.1 %collective-permute-done.2 = f32[2,2,16,768]{3,2,1,0:T(8,128)S(1)} collective-permute-done((f32[2,2,16,768]{3,2,1,0:T(8,128)S(1)}, f32[2,2,16,768]{3,2,1,0:T(8,128)S(1)}, u32[]{:S(2)}, u32[]{:S(2)}) %collective-permute-start.2) | collective-permute-done | bytes 196640 | tf_op jit(solution)/shard_map/ppermute | solution.py:55
  32.5 1.3 broadcast_in_dim.22
  33.7 5.6 %all-to-all-start = ((f32[4,128,768]{2,1,0:T(8,128)}), f32[4,128,768]{2,1,0:T(8,128)S(1)}, u32[]{:S(2)}, u32[]{:S(2)}) async-start(f32[4,128,768]{2,1,0:T(8,128)} %broadcast_in_dim.22), calls=%async_computation | async-start | bytes 3145728 | tf_op jit(solution)/shard_map/all_to_all | solution.py:57
  39.4 0.0 copy-done.3
  39.4 16.5 %all-to-all-done = f32[4,128,768]{2,1,0:T(8,128)S(1)} async-done(((f32[4,128,768]{2,1,0:T(8,128)}), f32[4,128,768]{2,1,0:T(8,128)S(1)}, u32[]{:S(2)}, u32[]{:S(2)}) %all-to-all-start) | async-done | bytes 1572896 | tf_op jit(solution)/shard_map/all_to_all | solution.py:57
  55.9 0.2 mul.62
  56.0 2.4 %fusion.1 = f32[8,64,384]{2,1,0:T(8,128)} fusion(f32[8,64,768]{2,1,0:T(8,128)S(1)} %bitcast.53, f32[384,768]{1,0:T(8,128)S(1)} %copy-done, f32[48,8,6,128]{3,2,1,0:T(8,128)S(1)} %bitcast.55), kind=kOutput, calls=%fused_computation.2 | convolution fusion | flops 906264576 | bytes 4718592 | tf_op jit(solution)/shard_map/dot_general | solution.py:72
  58.4 4.6 %all-to-all-start.1 = ((f32[8,64,384]{2,1,0:T(8,128)}), f32[8,64,384]{2,1,0:T(8,128)S(1)}, u32[]{:S(2)}, u32[]{:S(2)}) async-start(f32[8,64,384]{2,1,0:T(8,128)} %fusion.1), calls=%async_computation.1 | async-start | bytes 1572864 | tf_op jit(solution)/shard_map/all_to_all | solution.py:79
  63.0 0.1 dynamic-slice_convert_fusion
  63.1 0.0 copy-start.1
  63.2 6.6 %collective-permute-start.4 = (f32[256,384]{1,0:T(8,128)S(1)}, f32[256,384]{1,0:T(8,128)S(1)}, u32[]{:S(2)}, u32[]{:S(2)}) collective-permute-start(f32[256,384]{1,0:T(8,128)S(1)} %bitcast.57), channel_id=1, source_target_pairs={{0,0},{32,1},{64,2},{96,3},{128,4},{160,5},{192,6},{224,7},{256,8}... | collective-permute-start | bytes 1179656 | tf_op jit(solution)/shard_map/ppermute | solution.py:64
  69.8 9.6 %all-to-all-done.1 = f32[8,64,384]{2,1,0:T(8,128)S(1)} async-done(((f32[8,64,384]{2,1,0:T(8,128)}), f32[8,64,384]{2,1,0:T(8,128)S(1)}, u32[]{:S(2)}, u32[]{:S(2)}) %all-to-all-start.1) | async-done | bytes 786464 | tf_op jit(solution)/shard_map/all_to_all | solution.py:79
  79.5 7.1 %collective-permute-start.3 = (f32[32,384]{1,0:T(8,128)S(1)}, f32[32,384]{1,0:T(8,128)S(1)}, u32[]{:S(2)}, u32[]{:S(2)}) collective-permute-start(f32[32,384]{1,0:T(8,128)S(1)} %slice_select_fusion), channel_id=1, source_target_pairs={{0,2},{2,0},{1,3},{3,1},{4,6},{6,4},{5,7},{7,5},{8,10},{10,8},{9,1... | collective-permute-start | bytes 147464 | tf_op jit(solution)/shard_map/ppermute | solution.py:83
  86.6 0.1 broadcast_bitcast_fusion.1
  86.7 10.9 %collective-permute-done.3 = f32[32,384]{1,0:T(8,128)S(1)} collective-permute-done((f32[32,384]{1,0:T(8,128)S(1)}, f32[32,384]{1,0:T(8,128)S(1)}, u32[]{:S(2)}, u32[]{:S(2)}) %collective-permute-start.3) | collective-permute-done | bytes 49184 | tf_op jit(solution)/shard_map/ppermute | solution.py:83
  97.6 0.6 negate_bitcast_fusion
  98.2 0.0 collective-permute-done.4
  98.2 0.3 convolution_bitcast_fusion
  98.6 38.9 %all_to_all.20 = f32[32,1,256]{2,1,0:T(1,128)S(1)} all-to-all(f32[32,1,256]{2,1,0:T(1,128)S(1)} %copy.12), channel_id=1, replica_groups=mesh['x'=4,'zl'=8,'y'=4,'zh'=2,'core'=2] {'x','zl'}, dimensions={0} | all-to-all | bytes 65536 | tf_op jit(solution)/shard_map/all_to_all | solution.py:93
  137.4 0.1 reduce_sum.19
  137.5 15.8 %all_to_all.21 = f32[32,1,256]{2,1,0:T(1,128)S(1)} all-to-all(f32[32,1,256]{2,1,0:T(1,128)S(1)} %broadcast_in_dim.24), channel_id=1, replica_groups=mesh['x'=4,'zl'=8,'y'=4,'zh'=2,'core'=2] {'x','zl'}, dimensions={0} | all-to-all | bytes 65536 | tf_op jit(solution)/shard_map/all_to_all | solution.py:94
  153.3 0.0 copy-done.1
  153.3 0.6 bitcast_add_fusion
  (19 shorter events, 0.3 us)
Async XLA Ops:
  2.3 11.2 %collective-permute-start = (f32[16,768]{1,0:T(8,128)S(1)}, f32[16,768]{1,0:T(8,128)S(1)}, u32[]{:S(2)}, u32[]{:S(2)}) collective-permute-start(f32[16,768]{1,0:T(8,128)S(1)} %multiply_bitcast_fusion), channel_id=1, source_target_pairs={{0,64},{16,80},{32,96},{48,112},{64,0},{80,16},{96,32},{112,48},{1... | collective-permute-start | bytes 147464 | tf_op jit(solution)/shard_map/ppermute | solution.py:53
  14.3 10.4 %collective-permute-start.1 = (f32[2,16,768]{2,1,0:T(8,128)S(1)}, f32[2,16,768]{2,1,0:T(8,128)S(1)}, u32[]{:S(2)}, u32[]{:S(2)}) collective-permute-start(f32[2,16,768]{2,1,0:T(8,128)S(1)} %pad_maximum_fusion.2), channel_id=1, source_target_pairs={{0,32},{16,48},{32,0},{48,16},{64,96},{80,112},{96,64},{112,80},{1... | collective-permute-start | bytes 294920 | tf_op jit(solution)/shard_map/ppermute | solution.py:54
  24.7 7.7 %collective-permute-start.2 = (f32[2,2,16,768]{3,2,1,0:T(8,128)S(1)}, f32[2,2,16,768]{3,2,1,0:T(8,128)S(1)}, u32[]{:S(2)}, u32[]{:S(2)}) collective-permute-start(f32[2,2,16,768]{3,2,1,0:T(8,128)S(1)} %pad_maximum_fusion.1), channel_id=1, source_target_pairs={{0,16},{16,0},{32,48},{48,32},{64,80},{80,64},{96,112},{112,96},{1... | collective-permute-start | bytes 589832 | tf_op jit(solution)/shard_map/ppermute | solution.py:55
  33.7 5.6 %copy-start.3 = (s32[3,6]{1,0:T(4,128)S(1)}, s32[3,6]{1,0:T(4,128)}, u32[]{:S(2)}) copy-start(s32[3,6]{1,0:T(4,128)} %param.6) | copy-start | bytes 220
  33.7 22.1 %all-to-all-start = ((f32[4,128,768]{2,1,0:T(8,128)}), f32[4,128,768]{2,1,0:T(8,128)S(1)}, u32[]{:S(2)}, u32[]{:S(2)}) async-start(f32[4,128,768]{2,1,0:T(8,128)} %broadcast_in_dim.22), calls=%async_computation | async-start | bytes 3145728 | tf_op jit(solution)/shard_map/all_to_all | solution.py:57
  39.4 16.7 %copy-start = (f32[384,768]{1,0:T(8,128)S(1)}, f32[384,768]{1,0:T(8,128)}, u32[]{:S(2)}) copy-start(f32[384,768]{1,0:T(8,128)} %param.5) | copy-start | bytes 3538948
  58.4 4.6 %copy-start.2 = (s32[96,2]{0,1:T(2,128)S(1)}, s32[96,2]{0,1:T(2,128)}, u32[]{:S(2)}) copy-start(s32[96,2]{0,1:T(2,128)} %param.7) | copy-start | bytes 2308
  58.4 21.0 %all-to-all-start.1 = ((f32[8,64,384]{2,1,0:T(8,128)}), f32[8,64,384]{2,1,0:T(8,128)S(1)}, u32[]{:S(2)}, u32[]{:S(2)}) async-start(f32[8,64,384]{2,1,0:T(8,128)} %fusion.1), calls=%async_computation.1 | async-start | bytes 1572864 | tf_op jit(solution)/shard_map/all_to_all | solution.py:79
  63.1 90.1 %copy-start.1 = (f32[256,32]{0,1:T(8,128)S(1)}, f32[256,32]{0,1:T(8,128)}, u32[]{:S(2)}) copy-start(f32[256,32]{0,1:T(8,128)} %param.9) | copy-start | bytes 98308
  63.2 35.0 %collective-permute-start.4 = (f32[256,384]{1,0:T(8,128)S(1)}, f32[256,384]{1,0:T(8,128)S(1)}, u32[]{:S(2)}, u32[]{:S(2)}) collective-permute-start(f32[256,384]{1,0:T(8,128)S(1)} %bitcast.57), channel_id=1, source_target_pairs={{0,0},{32,1},{64,2},{96,3},{128,4},{160,5},{192,6},{224,7},{256,8}... | collective-permute-start | bytes 1179656 | tf_op jit(solution)/shard_map/ppermute | solution.py:64
  79.5 18.1 %collective-permute-start.3 = (f32[32,384]{1,0:T(8,128)S(1)}, f32[32,384]{1,0:T(8,128)S(1)}, u32[]{:S(2)}, u32[]{:S(2)}) collective-permute-start(f32[32,384]{1,0:T(8,128)S(1)} %slice_select_fusion), channel_id=1, source_target_pairs={{0,2},{2,0},{1,3},{3,1},{4,6},{6,4},{5,7},{7,5},{8,10},{10,8},{9,1... | collective-permute-start | bytes 147464 | tf_op jit(solution)/shard_map/ppermute | solution.py:83

commit v2 on v1

v2 whole, which is shorter than its diff:
```python
import jax
import jax.numpy as jnp
from jax import lax
from jax.sharding import Mesh, PartitionSpec as P


W = 256
BS = 128
ROW = ("x", "zl")
COL = ("y", "zh", "core")
SIZES = (4, 8, 4, 2, 2)
CLOSE = lax.Precision.HIGH


def flat(x, zl, y, zh, core):
    return (((x * 8 + zl) * 4 + y) * 2 + zh) * 2 + core


def row_block_pairs(turn):
    pairs = []
    for x in range(4):
        for zl in range(8):
            for y in range(4):
                for zh in range(2):
                    for core in range(2):
                        source = flat(y ^ turn, zh * 4 + core * 2 + (zl & 1), x, zl >> 2, (zl >> 1) & 1)
                        pairs.append((source, flat(x, zl, y, zh, core)))
    return pairs


def xor_pairs(size, step):
    return [(i, i ^ step) for i in range(size)]


def swapped(bit, first, second):
    return jnp.where(bit == 0, first, second), jnp.where(bit == 0, second, first)


def product(left, right):
    return lax.dot_general(
        left, right, (((1,), (1,)), ((), ())), precision=CLOSE, preferred_element_type=jnp.float32
    )


def copies(block, count, axes):
    return lax.all_to_all(jnp.broadcast_to(block[None], (count,) + block.shape), axes, 0, 0, tiled=True)


def body(ancestor, pattern, member, panel, diag_inv):
    x, zl = lax.axis_index("x"), lax.axis_index("zl")
    y, zh, core = lax.axis_index("y"), lax.axis_index("zh"), lax.axis_index("core")
    row, col = x * 8 + zl, (y * 2 + zh) * 2 + core
    bit2, bit1, bit0 = zl // 4, zl // 2 % 2, zl % 2
    row_blocks, col_blocks = pattern.shape
    rows, cols = ancestor.shape
    share = panel.shape[1]

    own = panel.T
    two = jnp.stack([own, lax.ppermute(own, "zl", xor_pairs(8, 4))])
    four = jnp.stack(swapped(bit1, two, lax.ppermute(two, "zl", xor_pairs(8, 2))))
    other_four = lax.ppermute(four, "zl", xor_pairs(8, 1))

    flags = member.astype(jnp.float32)
    keep_cols = lax.dynamic_slice_in_dim(flags, col * col_blocks, col_blocks, 0).T
    keep_cols = jnp.repeat(keep_cols, BS, axis=1)
    keep_rows = lax.dynamic_slice_in_dim(flags, row * row_blocks, row_blocks, 0)
    keep_rows = jnp.repeat(jnp.where(y // 2 == 0, keep_rows[:, 0], keep_rows[:, 1]), BS)
    weights = pattern.astype(jnp.float32)
    masked = (
        ancestor.reshape(row_blocks, BS, col_blocks, BS) * weights[:, None, :, None]
    ).reshape(rows, cols)

    full = copies(jnp.stack([four, other_four], axis=1).reshape(8 * share, cols), 4, "x")
    full = full.reshape(2, 16 * share, cols) * keep_cols[:, None, :]
    partial_sum = product(full.reshape(32 * share, cols), masked)
    lower, upper = swapped(bit2, four[:, 0], four[:, 1])
    other_lower, other_upper = swapped(bit2, other_four[:, 0], other_four[:, 1])
    lower = jnp.stack(swapped(bit0, lower, other_lower), axis=1)
    upper = jnp.stack(swapped(bit0, upper, other_upper), axis=1)
    ordered = jnp.stack([lower, upper]).reshape(8 * share, cols)
    half = lax.dynamic_slice_in_dim(ordered, bit0 * rows, rows, 1)
    normed = []
    for turn in (0, 1):
        normed.append(lax.ppermute(half, ROW + COL, row_block_pairs(turn)))

    pieces = partial_sum.reshape(8, 4 * share, rows)
    pieces = lax.all_to_all(pieces, ("y", "core"), 0, 0, tiled=True)
    pieces = pieces.reshape(8, 2, 2, share, rows)
    side = zh ^ bit2
    theirs = lax.dynamic_index_in_dim(pieces, 1 - side, 2, keepdims=False).sum(0).reshape(2 * share, rows)
    mine = lax.dynamic_index_in_dim(pieces, side, 2, keepdims=False).sum(0).reshape(2 * share, rows)
    arrived = lax.ppermute(theirs, "zh", xor_pairs(2, 1))
    def term_of(values):
        values = values * keep_rows[None, :]
        ends = swapped(y % 2, product(values, normed[0]), product(values, normed[1]))
        term = jnp.concatenate(ends, axis=1).reshape(2, share, W)
        return jnp.stack(swapped(bit0, term[0], term[1])).reshape(2 * share, W)

    term = jnp.concatenate(swapped(zh, term_of(mine), term_of(theirs)))
    owned = lax.all_to_all(term.reshape(64, 1, W), ("zh",) + ROW, 0, 0, tiled=True)
    owned = owned.sum(0)
    arrived, owned = lax.optimization_barrier((arrived, owned))
    total = copies(owned, 32, ROW)
    kept = ((mine + arrived) * keep_rows[None, :]).reshape(2, share, rows)
    kept = jnp.stack(swapped(bit0, kept[0], kept[1])).reshape(2 * share, rows)

    return (-kept).T, diag_inv + total.reshape(2 * share, W).T


def solution(mesh):
    fine = Mesh(mesh.devices.reshape(SIZES), ROW + COL)
    placed = (P(ROW, COL), P(ROW, COL), P(), P(COL, ROW), P(None, COL))
    return jax.shard_map(
        body,
        mesh=fine,
        in_specs=placed,
        out_specs=(P(ROW, COL), P(None, COL)),
        check_vma=False,
    )
```

time: 156 us -> 166 us (1.064)
  starting transfers between devices: 41 us -> 96 us
  blocking collectives: 54.6 us -> 0 us
  waiting for transfers between devices: 49.1 us -> 57.8 us
    all_to_all x2 -> x0, blocking collectives: 54.6 us -> none  [the longest x1 38.9 us: body(): owned = lax.all_to_all(term.reshape(32, 1, W), ROW, 0, 0, tiled=True).sum(0)]
    all_to_all x2 -> x4, starting transfers between devices: 10.2 us -> 55.9 us  [the longest x1 32.6 us: body(): lax.all_to_all(term.reshape(64, 1, W), ('zh',) + ROW, 0, 0, tiled=True)]
    ppermute x5 -> x6, starting transfers between devices: 30.8 us -> 40.1 us  [the longest x1 12.3 us: body(): arrived = lax.ppermute(theirs, 'zh', xor_pairs(2, 1))]
    all_to_all x2 -> x4, waiting for transfers between devices: 26.1 us -> 33.8 us  [the longest x2 26.2 us: copies(): lax.all_to_all(jnp.broadcast_to(block[None], (count,) + block.shape), axe...]
    ppermute x5 -> x6, waiting for transfers between devices: 23 us -> 24 us  [the longest x2 10.5 us: body(): normed.append(lax.ppermute(half, ROW + COL, row_block_pairs(turn)))]
  transfers between devices with their start and end apart: 7 -> 10, of which waited for: 6 -> 10; matrix products, arithmetic and copies ran while one was open for 1% -> 1% of each run, Pallas kernels for 0% -> 0%
where the time goes in v2:
time: 166 us; the launch traced here: 164 us
  starting transfers between devices  96 us (58%)
  waiting for transfers between devices  57.8 us (35%)
  other arithmetic  3.25 us (2%)
  matrix products  3.23 us (2%)
  local copies, waits for them, and re-layouts  3.14 us (2%)
    all_to_all x1, starting transfers between devices, body(): lax.all_to_all(term.reshape(64, 1, W), ('zh',) + ROW, 0, 0, tiled=True)  32.6 us
    all_to_all x2, waiting for transfers between devices, copies(): lax.all_to_all(jnp.broadcast_to(block[None], (count,) + block.shape), axe...  26.2 us
    all_to_all x2, starting transfers between devices, copies(): lax.all_to_all(jnp.broadcast_to(block[None], (count,) + block.shape), axe...  18.9 us
    ppermute x1, starting transfers between devices, body(): arrived = lax.ppermute(theirs, 'zh', xor_pairs(2, 1))  12.3 us
    ppermute x2, starting transfers between devices, body(): normed.append(lax.ppermute(half, ROW + COL, row_block_pairs(turn)))  10.6 us
    ppermute x2, waiting for transfers between devices, body(): normed.append(lax.ppermute(half, ROW + COL, row_block_pairs(turn)))  10.5 us
    ppermute x1, starting transfers between devices, body(): two = jnp.stack([own, lax.ppermute(own, 'zl', xor_pairs(8, 4))])  9.1 us
    all_to_all x1, waiting for transfers between devices, body(): pieces = lax.all_to_all(pieces, ('y', 'core'), 0, 0, tiled=True)  6.26 us
  transfers between devices with their start and end apart: 10, of which 10 were waited for; matrix products, arithmetic and copies ran while one was open for 1% of the time, Pallas kernels for 0%

profile of v2, /device:TPU:6, one launch (start us, length us, event | category | flops | bytes accessed | tf_op | source)
XLA Modules:
  0.0 164.3 jit_solution(3015467155669432804)
XLA Ops:
  0.6 9.1 %collective-permute-start = (f32[16,768]{1,0:T(8,128)}, f32[16,768]{1,0:T(8,128)S(1)}, u32[]{:S(2)}, u32[]{:S(2)}) collective-permute-start(f32[16,768]{1,0:T(8,128)} %bitcast.86), channel_id=1, source_target_pairs={{0,64},{16,80},{32,96},{48,112},{64,0},{80,16},{96,32},{112,48},{1... | collective-permute-start | bytes 147464 | tf_op jit(solution)/shard_map/ppermute | solution.py:59
  9.7 2.3 %collective-permute-done = f32[16,768]{1,0:T(8,128)S(1)} collective-permute-done((f32[16,768]{1,0:T(8,128)}, f32[16,768]{1,0:T(8,128)S(1)}, u32[]{:S(2)}, u32[]{:S(2)}) %collective-permute-start) | collective-permute-done | bytes 49184 | tf_op jit(solution)/shard_map/ppermute | solution.py:59
  12.0 0.8 pad_maximum_fusion.3
  12.8 5.4 %collective-permute-start.1 = (f32[2,16,768]{2,1,0:T(8,128)S(1)}, f32[2,16,768]{2,1,0:T(8,128)S(1)}, u32[]{:S(2)}, u32[]{:S(2)}) collective-permute-start(f32[2,16,768]{2,1,0:T(8,128)S(1)} %pad_maximum_fusion.3), channel_id=1, source_target_pairs={{0,32},{16,48},{32,0},{48,16},{64,96},{80,112},{96,64},{112,80},{1... | collective-permute-start | bytes 294920 | tf_op jit(solution)/shard_map/ppermute | solution.py:60
  18.3 5.0 %collective-permute-done.1 = f32[2,16,768]{2,1,0:T(8,128)S(1)} collective-permute-done((f32[2,16,768]{2,1,0:T(8,128)S(1)}, f32[2,16,768]{2,1,0:T(8,128)S(1)}, u32[]{:S(2)}, u32[]{:S(2)}) %collective-permute-start.1) | collective-permute-done | bytes 98336 | tf_op jit(solution)/shard_map/ppermute | solution.py:60
  23.3 0.8 select_bitcast_fusion.1
  24.2 2.6 %collective-permute-start.2 = (f32[2,2,16,768]{3,2,1,0:T(8,128)S(1)}, f32[2,2,16,768]{3,2,1,0:T(8,128)S(1)}, u32[]{:S(2)}, u32[]{:S(2)}) collective-permute-start(f32[2,2,16,768]{3,2,1,0:T(8,128)S(1)} %get-tuple-element.15), channel_id=1, source_target_pairs={{0,16},{16,0},{32,48},{48,32},{64,80},{80,64},{96,112},{112,96},{1... | collective-permute-start | bytes 589832 | tf_op jit(solution)/shard_map/ppermute | solution.py:61
  26.8 5.1 %collective-permute-done.2 = f32[2,2,16,768]{3,2,1,0:T(8,128)S(1)} collective-permute-done((f32[2,2,16,768]{3,2,1,0:T(8,128)S(1)}, f32[2,2,16,768]{3,2,1,0:T(8,128)S(1)}, u32[]{:S(2)}, u32[]{:S(2)}) %collective-permute-start.2) | collective-permute-done | bytes 196640 | tf_op jit(solution)/shard_map/ppermute | solution.py:61
  31.9 1.3 broadcast_in_dim.23
  33.2 5.5 %all-to-all-start = ((f32[4,128,768]{2,1,0:T(8,128)}), f32[4,128,768]{2,1,0:T(8,128)S(1)}, u32[]{:S(2)}, u32[]{:S(2)}) async-start(f32[4,128,768]{2,1,0:T(8,128)} %broadcast_in_dim.23), calls=%async_computation | async-start | bytes 3145728 | tf_op jit(solution)/shard_map/all_to_all | solution.py:46
  39.1 16.2 %all-to-all-done = f32[4,128,768]{2,1,0:T(8,128)S(1)} async-done(((f32[4,128,768]{2,1,0:T(8,128)}), f32[4,128,768]{2,1,0:T(8,128)S(1)}, u32[]{:S(2)}, u32[]{:S(2)}) %all-to-all-start) | async-done | bytes 1572896 | tf_op jit(solution)/shard_map/all_to_all | solution.py:46
  55.5 2.4 %fusion = f32[8,64,384]{2,1,0:T(8,128)} fusion(f32[8,64,768]{2,1,0:T(8,128)S(1)} %bitcast.77, f32[384,768]{1,0:T(8,128)S(1)} %copy-done, f32[48,8,6,128]{3,2,1,0:T(8,128)S(1)} %bitcast.78, f32[8,768]{1,0:T(8,128)S(1)} %mul.72), kind=kOutput, calls=%fused_computation | convolution fusion | flops 906657792 | bytes 4743168 | tf_op jit(solution)/shard_map/dot_general | solution.py:40
  57.9 4.5 %all-to-all-start.1 = ((f32[8,64,384]{2,1,0:T(8,128)}), f32[8,64,384]{2,1,0:T(8,128)S(1)}, u32[]{:S(2)}, u32[]{:S(2)}) async-start(f32[8,64,384]{2,1,0:T(8,128)} %fusion), calls=%async_computation.1 | async-start | bytes 1572864 | tf_op jit(solution)/shard_map/all_to_all | solution.py:87
  62.5 6.9 %collective-permute-start.5 = (f32[128,384]{1,0:T(8,128)S(1)}, f32[128,384]{1,0:T(8,128)S(1)}, u32[]{:S(2)}, u32[]{:S(2)}) collective-permute-start(f32[128,384]{1,0:T(8,128)S(1)} %constant_dynamic-slice_fusion), channel_id=1, source_target_pairs={{128,0},{160,1},{192,2},{224,3},{0,4},{32,5},{64,6},{96,7},{384,8}... | collective-permute-start | bytes 589832 | tf_op jit(solution)/shard_map/ppermute | solution.py:84
  69.4 3.7 %collective-permute-start.4 = (f32[128,384]{1,0:T(8,128)S(1)}, f32[128,384]{1,0:T(8,128)S(1)}, u32[]{:S(2)}, u32[]{:S(2)}) collective-permute-start(f32[128,384]{1,0:T(8,128)S(1)} %constant_dynamic-slice_fusion), channel_id=1, source_target_pairs={{0,0},{32,1},{64,2},{96,3},{128,4},{160,5},{192,6},{224,7},{256,8}... | collective-permute-start | bytes 589832 | tf_op jit(solution)/shard_map/ppermute | solution.py:84
  73.1 6.3 %all-to-all-done.1 = f32[8,64,384]{2,1,0:T(8,128)S(1)} async-done(((f32[8,64,384]{2,1,0:T(8,128)}), f32[8,64,384]{2,1,0:T(8,128)S(1)}, u32[]{:S(2)}, u32[]{:S(2)}) %all-to-all-start.1) | async-done | bytes 786464 | tf_op jit(solution)/shard_map/all_to_all | solution.py:87
  79.5 5.8 %collective-permute-done.5 = f32[128,384]{1,0:T(8,128)S(1)} collective-permute-done((f32[128,384]{1,0:T(8,128)S(1)}, f32[128,384]{1,0:T(8,128)S(1)}, u32[]{:S(2)}, u32[]{:S(2)}) %collective-permute-start.5) | collective-permute-done | bytes 196640 | tf_op jit(solution)/shard_map/ppermute | solution.py:84
  85.2 0.2 fusion.9
  85.5 0.2 fusion.24
  85.7 4.7 %collective-permute-done.4 = f32[128,384]{1,0:T(8,128)S(1)} collective-permute-done((f32[128,384]{1,0:T(8,128)S(1)}, f32[128,384]{1,0:T(8,128)S(1)}, u32[]{:S(2)}, u32[]{:S(2)}) %collective-permute-start.4) | collective-permute-done | bytes 196640 | tf_op jit(solution)/shard_map/ppermute | solution.py:84
  90.4 0.2 broadcast_select_fusion.9
  90.6 0.2 broadcast_select_fusion.7
  90.9 0.7 reshape.74
  91.6 32.6 %all-to-all-start.2 = ((f32[64,1,256]{2,1,0:T(1,128)}), f32[64,1,256]{2,1,0:T(1,128)S(1)}, u32[]{:S(2)}, u32[]{:S(2)}) async-start(f32[64,1,256]{2,1,0:T(1,128)} %reshape.74), calls=%async_computation.2 | async-start | bytes 131072 | tf_op jit(solution)/shard_map/all_to_all | solution.py:100
  124.1 12.3 %collective-permute-start.3 = (f32[32,384]{1,0:T(8,128)S(1)}, f32[32,384]{1,0:T(8,128)S(1)}, u32[]{:S(2)}, u32[]{:S(2)}) collective-permute-start(f32[32,384]{1,0:T(8,128)S(1)} %bitcast.85), channel_id=1, source_target_pairs={{0,2},{2,0},{1,3},{3,1},{4,6},{6,4},{5,7},{7,5},{8,10},{10,8},{9,1... | collective-permute-start | bytes 147464 | tf_op jit(solution)/shard_map/ppermute | solution.py:92
  136.5 1.3 all-to-all-done.2
  137.9 1.1 collective-permute-done.3
  139.0 0.6 broadcast_in_dim.27
  139.7 13.4 %all-to-all-start.3 = ((f32[32,1,256]{2,1,0:T(1,128)}), f32[32,1,256]{2,1,0:T(1,128)S(1)}, u32[]{:S(2)}, u32[]{:S(2)}) async-start(f32[32,1,256]{2,1,0:T(1,128)} %broadcast_in_dim.27), calls=%async_computation.3 | async-start | bytes 65536 | tf_op jit(solution)/shard_map/all_to_all | solution.py:46
  153.1 0.6 maximum_negate_fusion
  153.7 10.0 %all-to-all-done.3 = f32[32,1,256]{2,1,0:T(1,128)S(1)} async-done(((f32[32,1,256]{2,1,0:T(1,128)}), f32[32,1,256]{2,1,0:T(1,128)S(1)}, u32[]{:S(2)}, u32[]{:S(2)}) %all-to-all-start.3) | async-done | bytes 32800 | tf_op jit(solution)/shard_map/all_to_all | solution.py:46
  163.7 0.6 bitcast_add_fusion.1
  (35 shorter events, 0.9 us)
Async XLA Ops:
  0.6 11.4 %collective-permute-start = (f32[16,768]{1,0:T(8,128)}, f32[16,768]{1,0:T(8,128)S(1)}, u32[]{:S(2)}, u32[]{:S(2)}) collective-permute-start(f32[16,768]{1,0:T(8,128)} %bitcast.86), channel_id=1, source_target_pairs={{0,64},{16,80},{32,96},{48,112},{64,0},{80,16},{96,32},{112,48},{1... | collective-permute-start | bytes 147464 | tf_op jit(solution)/shard_map/ppermute | solution.py:59
  12.8 10.5 %collective-permute-start.1 = (f32[2,16,768]{2,1,0:T(8,128)S(1)}, f32[2,16,768]{2,1,0:T(8,128)S(1)}, u32[]{:S(2)}, u32[]{:S(2)}) collective-permute-start(f32[2,16,768]{2,1,0:T(8,128)S(1)} %pad_maximum_fusion.3), channel_id=1, source_target_pairs={{0,32},{16,48},{32,0},{48,16},{64,96},{80,112},{96,64},{112,80},{1... | collective-permute-start | bytes 294920 | tf_op jit(solution)/shard_map/ppermute | solution.py:60
  24.2 7.7 %collective-permute-start.2 = (f32[2,2,16,768]{3,2,1,0:T(8,128)S(1)}, f32[2,2,16,768]{3,2,1,0:T(8,128)S(1)}, u32[]{:S(2)}, u32[]{:S(2)}) collective-permute-start(f32[2,2,16,768]{3,2,1,0:T(8,128)S(1)} %get-tuple-element.15), channel_id=1, source_target_pairs={{0,16},{16,0},{32,48},{48,32},{64,80},{80,64},{96,112},{112,96},{1... | collective-permute-start | bytes 589832 | tf_op jit(solution)/shard_map/ppermute | solution.py:61
  33.2 5.5 %copy-start.3 = (s32[96,2]{0,1:T(2,128)S(1)}, s32[96,2]{0,1:T(2,128)}, u32[]{:S(2)}) copy-start(s32[96,2]{0,1:T(2,128)} %param.7) | copy-start | bytes 2308
  33.2 5.7 %copy-start.2 = (s32[3,6]{1,0:T(4,128)S(1)}, s32[3,6]{1,0:T(4,128)}, u32[]{:S(2)}) copy-start(s32[3,6]{1,0:T(4,128)} %param.6) | copy-start | bytes 220
  33.2 22.1 %all-to-all-start = ((f32[4,128,768]{2,1,0:T(8,128)}), f32[4,128,768]{2,1,0:T(8,128)S(1)}, u32[]{:S(2)}, u32[]{:S(2)}) async-start(f32[4,128,768]{2,1,0:T(8,128)} %broadcast_in_dim.23), calls=%async_computation | async-start | bytes 3145728 | tf_op jit(solution)/shard_map/all_to_all | solution.py:46
  38.7 16.8 %copy-start = (f32[384,768]{1,0:T(8,128)S(1)}, f32[384,768]{1,0:T(8,128)}, u32[]{:S(2)}) copy-start(f32[384,768]{1,0:T(8,128)} %param.5) | copy-start | bytes 3538948
  57.9 21.5 %all-to-all-start.1 = ((f32[8,64,384]{2,1,0:T(8,128)}), f32[8,64,384]{2,1,0:T(8,128)S(1)}, u32[]{:S(2)}, u32[]{:S(2)}) async-start(f32[8,64,384]{2,1,0:T(8,128)} %fusion), calls=%async_computation.1 | async-start | bytes 1572864 | tf_op jit(solution)/shard_map/all_to_all | solution.py:87
  62.5 22.8 %collective-permute-start.5 = (f32[128,384]{1,0:T(8,128)S(1)}, f32[128,384]{1,0:T(8,128)S(1)}, u32[]{:S(2)}, u32[]{:S(2)}) collective-permute-start(f32[128,384]{1,0:T(8,128)S(1)} %constant_dynamic-slice_fusion), channel_id=1, source_target_pairs={{128,0},{160,1},{192,2},{224,3},{0,4},{32,5},{64,6},{96,7},{384,8}... | collective-permute-start | bytes 589832 | tf_op jit(solution)/shard_map/ppermute | solution.py:84
  69.4 20.9 %collective-permute-start.4 = (f32[128,384]{1,0:T(8,128)S(1)}, f32[128,384]{1,0:T(8,128)S(1)}, u32[]{:S(2)}, u32[]{:S(2)}) collective-permute-start(f32[128,384]{1,0:T(8,128)S(1)} %constant_dynamic-slice_fusion), channel_id=1, source_target_pairs={{0,0},{32,1},{64,2},{96,3},{128,4},{160,5},{192,6},{224,7},{256,8}... | collective-permute-start | bytes 589832 | tf_op jit(solution)/shard_map/ppermute | solution.py:84
  79.4 84.3 %copy-start.1 = (f32[256,32]{0,1:T(8,128)S(1)}, f32[256,32]{0,1:T(8,128)}, u32[]{:S(2)}) copy-start(f32[256,32]{0,1:T(8,128)} %param.9) | copy-start | bytes 98308
  91.6 46.2 %all-to-all-start.2 = ((f32[64,1,256]{2,1,0:T(1,128)}), f32[64,1,256]{2,1,0:T(1,128)S(1)}, u32[]{:S(2)}, u32[]{:S(2)}) async-start(f32[64,1,256]{2,1,0:T(1,128)} %reshape.74), calls=%async_computation.2 | async-start | bytes 131072 | tf_op jit(solution)/shard_map/all_to_all | solution.py:100
  124.1 14.9 %collective-permute-start.3 = (f32[32,384]{1,0:T(8,128)S(1)}, f32[32,384]{1,0:T(8,128)S(1)}, u32[]{:S(2)}, u32[]{:S(2)}) collective-permute-start(f32[32,384]{1,0:T(8,128)S(1)} %bitcast.85), channel_id=1, source_target_pairs={{0,2},{2,0},{1,3},{3,1},{4,6},{6,4},{5,7},{7,5},{8,10},{10,8},{9,1... | collective-permute-start | bytes 147464 | tf_op jit(solution)/shard_map/ppermute | solution.py:92
  139.7 24.1 %all-to-all-start.3 = ((f32[32,1,256]{2,1,0:T(1,128)}), f32[32,1,256]{2,1,0:T(1,128)S(1)}, u32[]{:S(2)}, u32[]{:S(2)}) async-start(f32[32,1,256]{2,1,0:T(1,128)} %broadcast_in_dim.27), calls=%async_computation.3 | async-start | bytes 65536 | tf_op jit(solution)/shard_map/all_to_all | solution.py:46

commit v3 on v2

--- a/solution.py
+++ b/solution.py
@@ -4,7 +4,6 @@
 from jax.sharding import Mesh, PartitionSpec as P
 
 
-W = 256
 BS = 128
 ROW = ("x", "zl")
 COL = ("y", "zh", "core")
@@ -16,14 +15,14 @@
     return (((x * 8 + zl) * 4 + y) * 2 + zh) * 2 + core
 
 
-def row_block_pairs(turn):
+def row_block_pairs():
     pairs = []
     for x in range(4):
         for zl in range(8):
             for y in range(4):
                 for zh in range(2):
                     for core in range(2):
-                        source = flat(y ^ turn, zh * 4 + core * 2 + (zl & 1), x, zl >> 2, (zl >> 1) & 1)
+                        source = flat(y ^ core, zh * 4 + core * 2 + (zl & 1), x, zl >> 2, (zl >> 1) & 1)
                         pairs.append((source, flat(x, zl, y, zh, core)))
     return pairs
 
@@ -40,6 +39,11 @@
     return lax.dot_general(
         left, right, (((1,), (1,)), ((), ())), precision=CLOSE, preferred_element_type=jnp.float32
     )
+
+
+def four_sum(term, axis, size):
+    one, two, three = (lax.ppermute(term, axis, xor_pairs(size, k)) for k in (1, 2, 3))
+    return (term + one) + (two + three)
 
 
 def copies(block, count, axes):
@@ -79,32 +83,26 @@
     upper = jnp.stack(swapped(bit0, upper, other_upper), axis=1)
     ordered = jnp.stack([lower, upper]).reshape(8 * share, cols)
     half = lax.dynamic_slice_in_dim(ordered, bit0 * rows, rows, 1)
-    normed = []
-    for turn in (0, 1):
-        normed.append(lax.ppermute(half, ROW + COL, row_block_pairs(turn)))
+    normed = lax.ppermute(half, ROW + COL, row_block_pairs())
+    other_normed = lax.ppermute(normed, "core", xor_pairs(2, 1))
 
     pieces = partial_sum.reshape(8, 4 * share, rows)
     pieces = lax.all_to_all(pieces, ("y", "core"), 0, 0, tiled=True)
     pieces = pieces.reshape(8, 2, 2, share, rows)
     side = zh ^ bit2
-    theirs = lax.dynamic_index_in_dim(pieces, 1 - side, 2, keepdims=False).sum(0).reshape(2 * share, rows)
-    mine = lax.dynamic_index_in_dim(pieces, side, 2, keepdims=False).sum(0).reshape(2 * share, rows)
-    arrived = lax.ppermute(theirs, "zh", xor_pairs(2, 1))
-    def term_of(values):
-        values = values * keep_rows[None, :]
-        ends = swapped(y % 2, product(values, normed[0]), product(values, normed[1]))
-        term = jnp.concatenate(ends, axis=1).reshape(2, share, W)
-        return jnp.stack(swapped(bit0, term[0], term[1])).reshape(2 * share, W)
-
-    term = jnp.concatenate(swapped(zh, term_of(mine), term_of(theirs)))
-    owned = lax.all_to_all(term.reshape(64, 1, W), ("zh",) + ROW, 0, 0, tiled=True)
-    owned = owned.sum(0)
-    arrived, owned = lax.optimization_barrier((arrived, owned))
-    total = copies(owned, 32, ROW)
-    kept = ((mine + arrived) * keep_rows[None, :]).reshape(2, share, rows)
+    theirs = lax.dynamic_index_in_dim(pieces, 1 - side, 2, keepdims=False).sum(0)
+    mine = lax.dynamic_index_in_dim(pieces, side, 2, keepdims=False).sum(0)
+    theirs, mine = theirs.reshape(2 * share, rows), mine.reshape(2 * share, rows)
+    kept = (mine + lax.ppermute(theirs, "zh", xor_pairs(2, 1))) * keep_rows[None, :]
+    kept = kept.reshape(2, share, rows)
     kept = jnp.stack(swapped(bit0, kept[0], kept[1])).reshape(2 * share, rows)
 
-    return (-kept).T, diag_inv + total.reshape(2 * share, W).T
+    ends = swapped((y % 2) ^ core, product(kept, normed), product(kept, other_normed))
+    term = jnp.concatenate(ends, axis=1)
+    term = four_sum(term, "x", 4)
+    term = four_sum(term, "zl", 8)
+    term = term + lax.ppermute(term, "zl", xor_pairs(8, 4))
+    return (-kept).T, diag_inv + term.T
 
 
 def solution(mesh):

time: 166 us -> 138 us (0.83)
  starting transfers between devices: 96 us -> 73.6 us
  waiting for transfers between devices: 57.8 us -> 55.3 us
    all_to_all x1 -> x0, starting transfers between devices: 32.6 us -> none  [body(): lax.all_to_all(term.reshape(64, 1, W), ('zh',) + ROW, 0, 0, tiled=True)]
    ppermute x3 -> x10, starting transfers between devices: 22.9 us -> 46.5 us  [the longest x6 27.2 us: four_sum(): lax.ppermute(term, axis, xor_pairs(size, k))]
    all_to_all x2 -> x1, starting transfers between devices: 18.9 us -> 5.5 us  [copies(): lax.all_to_all(jnp.broadcast_to(block[None], (count,) + block.shape), axe...]
    all_to_all x2 -> x1, waiting for transfers between devices: 26.2 us -> 16.3 us  [copies(): lax.all_to_all(jnp.broadcast_to(block[None], (count,) + block.shape), axe...]
    ppermute x3 -> x10, waiting for transfers between devices: 11.6 us -> 17.5 us  [the longest x1 5.88 us: body(): lax.ppermute(theirs, 'zh', xor_pairs(2, 1))]
    all_to_all x1, waiting for transfers between devices: 6.26 us -> 9.09 us  [body(): pieces = lax.all_to_all(pieces, ('y', 'core'), 0, 0, tiled=True)]
  transfers between devices with their start and end apart: 10 -> 15, of which waited for: 10 -> 9; matrix products, arithmetic and copies ran while one was open for 1% -> 1% of each run, Pallas kernels for 0% -> 0%
where the time goes in v3:
time: 138 us
  starting transfers between devices  73.6 us (53%)
  waiting for transfers between devices  55.3 us (40%)
  other arithmetic  3.15 us (2%)
  matrix products  2.79 us (2%)
  local copies, waits for them, and re-layouts  1.82 us (1%)
    ppermute x6, starting transfers between devices, four_sum(): lax.ppermute(term, axis, xor_pairs(size, k))  27.2 us
    all_to_all x1, waiting for transfers between devices, copies(): lax.all_to_all(jnp.broadcast_to(block[None], (count,) + block.shape), axe...  16.3 us
    ppermute x1, starting transfers between devices, body(): two = jnp.stack([own, lax.ppermute(own, 'zl', xor_pairs(8, 4))])  9.1 us
    all_to_all x1, waiting for transfers between devices, body(): pieces = lax.all_to_all(pieces, ('y', 'core'), 0, 0, tiled=True)  9.09 us
    ppermute x1, starting transfers between devices, body(): lax.ppermute(theirs, 'zh', xor_pairs(2, 1))  7.45 us
    ppermute x1, starting transfers between devices, body(): normed = lax.ppermute(half, ROW + COL, row_block_pairs())  6.65 us
    ppermute x1, waiting for transfers between devices, body(): lax.ppermute(theirs, 'zh', xor_pairs(2, 1))  5.88 us
    ppermute x1, waiting for transfers between devices, body(): term = term + lax.ppermute(term, 'zl', xor_pairs(8, 4))  5.84 us
  transfers between devices with their start and end apart: 15, of which 9 were waited for; matrix products, arithmetic and copies ran while one was open for 1% of the time, Pallas kernels for 0%

profile of v3, /device:TPU:6, one launch (start us, length us, event | category | flops | bytes accessed | tf_op | source)
XLA Modules:
  0.0 137.6 jit_solution(10244093108612336674)
XLA Ops:
  0.6 9.1 %collective-permute-start = (f32[16,768]{1,0:T(8,128)}, f32[16,768]{1,0:T(8,128)S(1)}, u32[]{:S(2)}, u32[]{:S(2)}) collective-permute-start(f32[16,768]{1,0:T(8,128)} %bitcast.69), channel_id=1, source_target_pairs={{0,64},{16,80},{32,96},{48,112},{64,0},{80,16},{96,32},{112,48},{1... | collective-permute-start | bytes 147464 | tf_op jit(solution)/shard_map/ppermute | solution.py:63
  9.7 2.3 %collective-permute-done = f32[16,768]{1,0:T(8,128)S(1)} collective-permute-done((f32[16,768]{1,0:T(8,128)}, f32[16,768]{1,0:T(8,128)S(1)}, u32[]{:S(2)}, u32[]{:S(2)}) %collective-permute-start) | collective-permute-done | bytes 49184 | tf_op jit(solution)/shard_map/ppermute | solution.py:63
  12.0 0.8 pad_maximum_fusion.3
  12.8 5.4 %collective-permute-start.1 = (f32[2,16,768]{2,1,0:T(8,128)S(1)}, f32[2,16,768]{2,1,0:T(8,128)S(1)}, u32[]{:S(2)}, u32[]{:S(2)}) collective-permute-start(f32[2,16,768]{2,1,0:T(8,128)S(1)} %pad_maximum_fusion.3), channel_id=1, source_target_pairs={{0,32},{16,48},{32,0},{48,16},{64,96},{80,112},{96,64},{112,80},{1... | collective-permute-start | bytes 294920 | tf_op jit(solution)/shard_map/ppermute | solution.py:64
  18.3 5.0 %collective-permute-done.1 = f32[2,16,768]{2,1,0:T(8,128)S(1)} collective-permute-done((f32[2,16,768]{2,1,0:T(8,128)S(1)}, f32[2,16,768]{2,1,0:T(8,128)S(1)}, u32[]{:S(2)}, u32[]{:S(2)}) %collective-permute-start.1) | collective-permute-done | bytes 98336 | tf_op jit(solution)/shard_map/ppermute | solution.py:64
  23.3 0.8 select_bitcast_fusion.1
  24.2 2.6 %collective-permute-start.2 = (f32[2,2,16,768]{3,2,1,0:T(8,128)S(1)}, f32[2,2,16,768]{3,2,1,0:T(8,128)S(1)}, u32[]{:S(2)}, u32[]{:S(2)}) collective-permute-start(f32[2,2,16,768]{3,2,1,0:T(8,128)S(1)} %get-tuple-element.11), channel_id=1, source_target_pairs={{0,16},{16,0},{32,48},{48,32},{64,80},{80,64},{96,112},{112,96},{1... | collective-permute-start | bytes 589832 | tf_op jit(solution)/shard_map/ppermute | solution.py:65
  26.8 5.1 %collective-permute-done.2 = f32[2,2,16,768]{3,2,1,0:T(8,128)S(1)} collective-permute-done((f32[2,2,16,768]{3,2,1,0:T(8,128)S(1)}, f32[2,2,16,768]{3,2,1,0:T(8,128)S(1)}, u32[]{:S(2)}, u32[]{:S(2)}) %collective-permute-start.2) | collective-permute-done | bytes 196640 | tf_op jit(solution)/shard_map/ppermute | solution.py:65
  31.9 1.3 broadcast_in_dim.15
  33.2 5.5 %all-to-all-start = ((f32[4,128,768]{2,1,0:T(8,128)}), f32[4,128,768]{2,1,0:T(8,128)S(1)}, u32[]{:S(2)}, u32[]{:S(2)}) async-start(f32[4,128,768]{2,1,0:T(8,128)} %broadcast_in_dim.15), calls=%async_computation | async-start | bytes 3145728 | tf_op jit(solution)/shard_map/all_to_all | solution.py:50
  39.0 16.3 %all-to-all-done = f32[4,128,768]{2,1,0:T(8,128)S(1)} async-done(((f32[4,128,768]{2,1,0:T(8,128)}), f32[4,128,768]{2,1,0:T(8,128)S(1)}, u32[]{:S(2)}, u32[]{:S(2)}) %all-to-all-start) | async-done | bytes 1572896 | tf_op jit(solution)/shard_map/all_to_all | solution.py:50
  55.5 2.4 %fusion = f32[8,64,384]{2,1,0:T(8,128)} fusion(f32[8,64,768]{2,1,0:T(8,128)S(1)} %bitcast.61, f32[384,768]{1,0:T(8,128)S(1)} %copy-done, f32[48,8,6,128]{3,2,1,0:T(8,128)S(1)} %bitcast.62, f32[8,768]{1,0:T(8,128)S(1)} %mul.60), kind=kOutput, calls=%fused_computation | convolution fusion | flops 906657792 | bytes 4743168 | tf_op jit(solution)/shard_map/dot_general | solution.py:39
  57.9 4.5 %all-to-all-start.1 = ((f32[8,64,384]{2,1,0:T(8,128)}), f32[8,64,384]{2,1,0:T(8,128)S(1)}, u32[]{:S(2)}, u32[]{:S(2)}) async-start(f32[8,64,384]{2,1,0:T(8,128)} %fusion), calls=%async_computation.1 | async-start | bytes 1572864 | tf_op jit(solution)/shard_map/all_to_all | solution.py:90
  62.5 6.6 %collective-permute-start.4 = (f32[128,384]{1,0:T(8,128)S(1)}, f32[128,384]{1,0:T(8,128)S(1)}, u32[]{:S(2)}, u32[]{:S(2)}) collective-permute-start(f32[128,384]{1,0:T(8,128)S(1)} %constant_dynamic-slice_fusion), channel_id=1, source_target_pairs={{0,0},{160,1},{64,2},{224,3},{128,4},{32,5},{192,6},{96,7},{256,8}... | collective-permute-start | bytes 589832 | tf_op jit(solution)/shard_map/ppermute | solution.py:86
  69.2 9.1 %all-to-all-done.1 = f32[8,64,384]{2,1,0:T(8,128)S(1)} async-done(((f32[8,64,384]{2,1,0:T(8,128)}), f32[8,64,384]{2,1,0:T(8,128)S(1)}, u32[]{:S(2)}, u32[]{:S(2)}) %all-to-all-start.1) | async-done | bytes 786464 | tf_op jit(solution)/shard_map/all_to_all | solution.py:90
  78.3 7.4 %collective-permute-start.3 = (f32[32,384]{1,0:T(8,128)S(1)}, f32[32,384]{1,0:T(8,128)S(1)}, u32[]{:S(2)}, u32[]{:S(2)}) collective-permute-start(f32[32,384]{1,0:T(8,128)S(1)} %bitcast.74), channel_id=1, source_target_pairs={{0,2},{2,0},{1,3},{3,1},{4,6},{6,4},{5,7},{7,5},{8,10},{10,8},{9,1... | collective-permute-start | bytes 147464 | tf_op jit(solution)/shard_map/ppermute | solution.py:96
  85.9 1.9 %collective-permute-start.5 = (f32[128,384]{1,0:T(8,128)S(1)}, f32[128,384]{1,0:T(8,128)S(1)}, u32[]{:S(2)}, u32[]{:S(2)}) collective-permute-start(f32[128,384]{1,0:T(8,128)S(1)} %collective-permute-done.4), channel_id=1, source_target_pairs={{0,1},{1,0},{2,3},{3,2},{4,5},{5,4},{6,7},{7,6},{8,9},{9,8},{10,11... | collective-permute-start | bytes 589832 | tf_op jit(solution)/shard_map/ppermute | solution.py:87
  87.8 5.9 %collective-permute-done.3 = f32[32,384]{1,0:T(8,128)S(1)} collective-permute-done((f32[32,384]{1,0:T(8,128)S(1)}, f32[32,384]{1,0:T(8,128)S(1)}, u32[]{:S(2)}, u32[]{:S(2)}) %collective-permute-start.3) | collective-permute-done | bytes 49184 | tf_op jit(solution)/shard_map/ppermute | solution.py:96
  93.7 0.2 fusion.14
  93.9 0.2 broadcast_select_fusion.7
  94.2 6.9 %collective-permute-start.7 = (f32[32,256]{1,0:T(8,128)S(1)}, f32[32,256]{1,0:T(8,128)S(1)}, u32[]{:S(2)}, u32[]{:S(2)}) collective-permute-start(f32[32,256]{1,0:T(8,128)S(1)} %pad_maximum_fusion.5), channel_id=1, source_target_pairs={{0,256},{128,384},{256,0},{384,128},{1,257},{129,385},{257,1},{385... | collective-permute-start | bytes 98312 | tf_op jit(solution)/shard_map/ppermute | solution.py:45
  101.1 8.2 %collective-permute-start.8 = (f32[32,256]{1,0:T(8,128)S(1)}, f32[32,256]{1,0:T(8,128)S(1)}, u32[]{:S(2)}, u32[]{:S(2)}) collective-permute-start(f32[32,256]{1,0:T(8,128)S(1)} %pad_maximum_fusion.5), channel_id=1, source_target_pairs={{0,384},{128,256},{256,128},{384,0},{1,385},{129,257},{257,129},{3... | collective-permute-start | bytes 98312 | tf_op jit(solution)/shard_map/ppermute | solution.py:45
  109.4 1.9 %collective-permute-start.6 = (f32[32,256]{1,0:T(8,128)S(1)}, f32[32,256]{1,0:T(8,128)S(1)}, u32[]{:S(2)}, u32[]{:S(2)}) collective-permute-start(f32[32,256]{1,0:T(8,128)S(1)} %pad_maximum_fusion.5), channel_id=1, source_target_pairs={{0,128},{128,0},{256,384},{384,256},{1,129},{129,1},{257,385},{385... | collective-permute-start | bytes 98312 | tf_op jit(solution)/shard_map/ppermute | solution.py:45
  111.3 3.9 %collective-permute-done.6 = f32[32,256]{1,0:T(8,128)S(1)} collective-permute-done((f32[32,256]{1,0:T(8,128)S(1)}, f32[32,256]{1,0:T(8,128)S(1)}, u32[]{:S(2)}, u32[]{:S(2)}) %collective-permute-start.6) | collective-permute-done | bytes 32800 | tf_op jit(solution)/shard_map/ppermute | solution.py:45
  115.2 1.9 %collective-permute-start.11 = (f32[32,256]{1,0:T(8,128)S(1)}, f32[32,256]{1,0:T(8,128)S(1)}, u32[]{:S(2)}, u32[]{:S(2)}) collective-permute-start(f32[32,256]{1,0:T(8,128)S(1)} %add_add_fusion.1), channel_id=1, source_target_pairs={{0,48},{16,32},{32,16},{48,0},{64,112},{80,96},{96,80},{112,64},{1... | collective-permute-start | bytes 98312 | tf_op jit(solution)/shard_map/ppermute | solution.py:45
  117.1 4.4 %collective-permute-start.10 = (f32[32,256]{1,0:T(8,128)S(1)}, f32[32,256]{1,0:T(8,128)S(1)}, u32[]{:S(2)}, u32[]{:S(2)}) collective-permute-start(f32[32,256]{1,0:T(8,128)S(1)} %add_add_fusion.1), channel_id=1, source_target_pairs={{0,32},{16,48},{32,0},{48,16},{64,96},{80,112},{96,64},{112,80},{1... | collective-permute-start | bytes 98312 | tf_op jit(solution)/shard_map/ppermute | solution.py:45
  121.5 3.8 %collective-permute-start.9 = (f32[32,256]{1,0:T(8,128)S(1)}, f32[32,256]{1,0:T(8,128)S(1)}, u32[]{:S(2)}, u32[]{:S(2)}) collective-permute-start(f32[32,256]{1,0:T(8,128)S(1)} %add_add_fusion.1), channel_id=1, source_target_pairs={{0,16},{16,0},{32,48},{48,32},{64,80},{80,64},{96,112},{112,96},{1... | collective-permute-start | bytes 98312 | tf_op jit(solution)/shard_map/ppermute | solution.py:45
  125.3 1.9 %collective-permute-done.9 = f32[32,256]{1,0:T(8,128)S(1)} collective-permute-done((f32[32,256]{1,0:T(8,128)S(1)}, f32[32,256]{1,0:T(8,128)S(1)}, u32[]{:S(2)}, u32[]{:S(2)}) %collective-permute-start.9) | collective-permute-done | bytes 32800 | tf_op jit(solution)/shard_map/ppermute | solution.py:45
  127.3 3.2 %collective-permute-start.12 = (f32[32,256]{1,0:T(8,128)S(1)}, f32[32,256]{1,0:T(8,128)S(1)}, u32[]{:S(2)}, u32[]{:S(2)}) collective-permute-start(f32[32,256]{1,0:T(8,128)S(1)} %add_add_fusion), channel_id=1, source_target_pairs={{0,64},{16,80},{32,96},{48,112},{64,0},{80,16},{96,32},{112,48},{1... | collective-permute-start | bytes 98312 | tf_op jit(solution)/shard_map/ppermute | solution.py:104
  130.5 0.6 negate_bitcast_fusion
  131.2 5.8 %collective-permute-done.12 = f32[32,256]{1,0:T(8,128)S(1)} collective-permute-done((f32[32,256]{1,0:T(8,128)S(1)}, f32[32,256]{1,0:T(8,128)S(1)}, u32[]{:S(2)}, u32[]{:S(2)}) %collective-permute-start.12) | collective-permute-done | bytes 32800 | tf_op jit(solution)/shard_map/ppermute | solution.py:104
  137.0 0.6 bitcast_add_fusion.1
  (39 shorter events, 0.8 us)
Async XLA Ops:
  0.6 11.4 %collective-permute-start = (f32[16,768]{1,0:T(8,128)}, f32[16,768]{1,0:T(8,128)S(1)}, u32[]{:S(2)}, u32[]{:S(2)}) collective-permute-start(f32[16,768]{1,0:T(8,128)} %bitcast.69), channel_id=1, source_target_pairs={{0,64},{16,80},{32,96},{48,112},{64,0},{80,16},{96,32},{112,48},{1... | collective-permute-start | bytes 147464 | tf_op jit(solution)/shard_map/ppermute | solution.py:63
  12.8 10.5 %collective-permute-start.1 = (f32[2,16,768]{2,1,0:T(8,128)S(1)}, f32[2,16,768]{2,1,0:T(8,128)S(1)}, u32[]{:S(2)}, u32[]{:S(2)}) collective-permute-start(f32[2,16,768]{2,1,0:T(8,128)S(1)} %pad_maximum_fusion.3), channel_id=1, source_target_pairs={{0,32},{16,48},{32,0},{48,16},{64,96},{80,112},{96,64},{112,80},{1... | collective-permute-start | bytes 294920 | tf_op jit(solution)/shard_map/ppermute | solution.py:64
  24.2 7.7 %collective-permute-start.2 = (f32[2,2,16,768]{3,2,1,0:T(8,128)S(1)}, f32[2,2,16,768]{3,2,1,0:T(8,128)S(1)}, u32[]{:S(2)}, u32[]{:S(2)}) collective-permute-start(f32[2,2,16,768]{3,2,1,0:T(8,128)S(1)} %get-tuple-element.11), channel_id=1, source_target_pairs={{0,16},{16,0},{32,48},{48,32},{64,80},{80,64},{96,112},{112,96},{1... | collective-permute-start | bytes 589832 | tf_op jit(solution)/shard_map/ppermute | solution.py:65
  33.2 5.5 %copy-start.3 = (s32[96,2]{0,1:T(2,128)S(1)}, s32[96,2]{0,1:T(2,128)}, u32[]{:S(2)}) copy-start(s32[96,2]{0,1:T(2,128)} %param.7) | copy-start | bytes 2308
  33.2 5.5 %copy-start.2 = (s32[3,6]{1,0:T(4,128)S(1)}, s32[3,6]{1,0:T(4,128)}, u32[]{:S(2)}) copy-start(s32[3,6]{1,0:T(4,128)} %param.6) | copy-start | bytes 220
  33.2 22.1 %all-to-all-start = ((f32[4,128,768]{2,1,0:T(8,128)}), f32[4,128,768]{2,1,0:T(8,128)S(1)}, u32[]{:S(2)}, u32[]{:S(2)}) async-start(f32[4,128,768]{2,1,0:T(8,128)} %broadcast_in_dim.15), calls=%async_computation | async-start | bytes 3145728 | tf_op jit(solution)/shard_map/all_to_all | solution.py:50
  38.7 16.8 %copy-start = (f32[384,768]{1,0:T(8,128)S(1)}, f32[384,768]{1,0:T(8,128)}, u32[]{:S(2)}) copy-start(f32[384,768]{1,0:T(8,128)} %param.5) | copy-start | bytes 3538948
  57.9 20.4 %all-to-all-start.1 = ((f32[8,64,384]{2,1,0:T(8,128)}), f32[8,64,384]{2,1,0:T(8,128)S(1)}, u32[]{:S(2)}, u32[]{:S(2)}) async-start(f32[8,64,384]{2,1,0:T(8,128)} %fusion), calls=%async_computation.1 | async-start | bytes 1572864 | tf_op jit(solution)/shard_map/all_to_all | solution.py:90
  62.4 74.6 %copy-start.1 = (f32[256,32]{0,1:T(8,128)S(1)}, f32[256,32]{0,1:T(8,128)}, u32[]{:S(2)}) copy-start(f32[256,32]{0,1:T(8,128)} %param.9) | copy-start | bytes 98308
  62.5 23.3 %collective-permute-start.4 = (f32[128,384]{1,0:T(8,128)S(1)}, f32[128,384]{1,0:T(8,128)S(1)}, u32[]{:S(2)}, u32[]{:S(2)}) collective-permute-start(f32[128,384]{1,0:T(8,128)S(1)} %constant_dynamic-slice_fusion), channel_id=1, source_target_pairs={{0,0},{160,1},{64,2},{224,3},{128,4},{32,5},{192,6},{96,7},{256,8}... | collective-permute-start | bytes 589832 | tf_op jit(solution)/shard_map/ppermute | solution.py:86
  78.3 15.3 %collective-permute-start.3 = (f32[32,384]{1,0:T(8,128)S(1)}, f32[32,384]{1,0:T(8,128)S(1)}, u32[]{:S(2)}, u32[]{:S(2)}) collective-permute-start(f32[32,384]{1,0:T(8,128)S(1)} %bitcast.74), channel_id=1, source_target_pairs={{0,2},{2,0},{1,3},{3,1},{4,6},{6,4},{5,7},{7,5},{8,10},{10,8},{9,1... | collective-permute-start | bytes 147464 | tf_op jit(solution)/shard_map/ppermute | solution.py:96
  85.9 8.1 %collective-permute-start.5 = (f32[128,384]{1,0:T(8,128)S(1)}, f32[128,384]{1,0:T(8,128)S(1)}, u32[]{:S(2)}, u32[]{:S(2)}) collective-permute-start(f32[128,384]{1,0:T(8,128)S(1)} %collective-permute-done.4), channel_id=1, source_target_pairs={{0,1},{1,0},{2,3},{3,2},{4,5},{5,4},{6,7},{7,6},{8,9},{9,8},{10,11... | collective-permute-start | bytes 589832 | tf_op jit(solution)/shard_map/ppermute | solution.py:87
  94.2 17.1 %collective-permute-start.7 = (f32[32,256]{1,0:T(8,128)S(1)}, f32[32,256]{1,0:T(8,128)S(1)}, u32[]{:S(2)}, u32[]{:S(2)}) collective-permute-start(f32[32,256]{1,0:T(8,128)S(1)} %pad_maximum_fusion.5), channel_id=1, source_target_pairs={{0,256},{128,384},{256,0},{384,128},{1,257},{129,385},{257,1},{385... | collective-permute-start | bytes 98312 | tf_op jit(solution)/shard_map/ppermute | solution.py:45
  101.1 10.2 %collective-permute-start.8 = (f32[32,256]{1,0:T(8,128)S(1)}, f32[32,256]{1,0:T(8,128)S(1)}, u32[]{:S(2)}, u32[]{:S(2)}) collective-permute-start(f32[32,256]{1,0:T(8,128)S(1)} %pad_maximum_fusion.5), channel_id=1, source_target_pairs={{0,384},{128,256},{256,128},{384,0},{1,385},{129,257},{257,129},{3... | collective-permute-start | bytes 98312 | tf_op jit(solution)/shard_map/ppermute | solution.py:45
  109.4 5.8 %collective-permute-start.6 = (f32[32,256]{1,0:T(8,128)S(1)}, f32[32,256]{1,0:T(8,128)S(1)}, u32[]{:S(2)}, u32[]{:S(2)}) collective-permute-start(f32[32,256]{1,0:T(8,128)S(1)} %pad_maximum_fusion.5), channel_id=1, source_target_pairs={{0,128},{128,0},{256,384},{384,256},{1,129},{129,1},{257,385},{385... | collective-permute-start | bytes 98312 | tf_op jit(solution)/shard_map/ppermute | solution.py:45
  115.2 10.1 %collective-permute-start.11 = (f32[32,256]{1,0:T(8,128)S(1)}, f32[32,256]{1,0:T(8,128)S(1)}, u32[]{:S(2)}, u32[]{:S(2)}) collective-permute-start(f32[32,256]{1,0:T(8,128)S(1)} %add_add_fusion.1), channel_id=1, source_target_pairs={{0,48},{16,32},{32,16},{48,0},{64,112},{80,96},{96,80},{112,64},{1... | collective-permute-start | bytes 98312 | tf_op jit(solution)/shard_map/ppermute | solution.py:45
  117.1 8.2 %collective-permute-start.10 = (f32[32,256]{1,0:T(8,128)S(1)}, f32[32,256]{1,0:T(8,128)S(1)}, u32[]{:S(2)}, u32[]{:S(2)}) collective-permute-start(f32[32,256]{1,0:T(8,128)S(1)} %add_add_fusion.1), channel_id=1, source_target_pairs={{0,32},{16,48},{32,0},{48,16},{64,96},{80,112},{96,64},{112,80},{1... | collective-permute-start | bytes 98312 | tf_op jit(solution)/shard_map/ppermute | solution.py:45
  121.5 5.8 %collective-permute-start.9 = (f32[32,256]{1,0:T(8,128)S(1)}, f32[32,256]{1,0:T(8,128)S(1)}, u32[]{:S(2)}, u32[]{:S(2)}) collective-permute-start(f32[32,256]{1,0:T(8,128)S(1)} %add_add_fusion.1), channel_id=1, source_target_pairs={{0,16},{16,0},{32,48},{48,32},{64,80},{80,64},{96,112},{112,96},{1... | collective-permute-start | bytes 98312 | tf_op jit(solution)/shard_map/ppermute | solution.py:45
  127.3 9.7 %collective-permute-start.12 = (f32[32,256]{1,0:T(8,128)S(1)}, f32[32,256]{1,0:T(8,128)S(1)}, u32[]{:S(2)}, u32[]{:S(2)}) collective-permute-start(f32[32,256]{1,0:T(8,128)S(1)} %add_add_fusion), channel_id=1, source_target_pairs={{0,64},{16,80},{32,96},{48,112},{64,0},{80,16},{96,32},{112,48},{1... | collective-permute-start | bytes 98312 | tf_op jit(solution)/shard_map/ppermute | solution.py:104

commit v4 on v3

v4 whole, which is shorter than its diff:
```python
import jax
import jax.numpy as jnp
from jax import lax
from jax.sharding import Mesh, PartitionSpec as P


W = 256
BS = 128
ROW = ("x", "zq", "zm", "z0")
COL = ("y", "zh", "core")
SIZES = (4, 2, 2, 2, 4, 2, 2)
CLOSE = lax.Precision.HIGH


def flat(*place):
    index = 0
    for size, at in zip(SIZES, place):
        index = index * size + at
    return index


def row_block_pairs():
    pairs = []
    for target in range(512):
        rest, place = target, []
        for size in reversed(SIZES):
            place.insert(0, rest % size)
            rest //= size
        x, zq, zm, z0, y, zh, core = place
        pairs.append((flat(y ^ core, zh, core, z0, x, zq, zm), target))
    return pairs


def product(left, right):
    return lax.dot_general(
        left, right, (((1,), (1,)), ((), ())), precision=CLOSE, preferred_element_type=jnp.float32
    )


def copies(block, count, axes):
    return lax.all_to_all(jnp.broadcast_to(block[None], (count,) + block.shape), axes, 0, 0, tiled=True)


def body(ancestor, pattern, member, panel, diag_inv):
    at = {name: lax.axis_index(name) for name in ROW + COL}
    y, zh, core, z0 = at["y"], at["zh"], at["core"], at["z0"]
    row = at["x"] * 8 + at["zq"] * 4 + at["zm"] * 2 + z0
    col = (y * 2 + zh) * 2 + core
    row_blocks, col_blocks = pattern.shape
    rows, cols = ancestor.shape
    share = panel.shape[1]

    flags = member.astype(jnp.float32)
    keep_cols = lax.dynamic_slice_in_dim(flags, col * col_blocks, col_blocks, 0).T
    keep_cols = jnp.repeat(keep_cols, BS, axis=1)
    keep_rows = lax.dynamic_slice_in_dim(flags, row * row_blocks, row_blocks, 0)
    keep_rows = jnp.repeat(jnp.where(y // 2 == 0, keep_rows[:, 0], keep_rows[:, 1]), BS)
    weights = pattern.astype(jnp.float32)
    masked = (
        ancestor.reshape(row_blocks, BS, col_blocks, BS) * weights[:, None, :, None]
    ).reshape(rows, cols)

    four = copies(panel.T, 4, ("zq", "zm"))
    full = copies(four.reshape(4 * share, cols), 8, ("x", "z0"))
    kept_cols = full.reshape(2, 16 * share, cols) * keep_cols[:, None, :]
    partial_sum = product(kept_cols.reshape(32 * share, cols), masked)
    pieces = partial_sum.reshape(4, 2, 2, 2, share, rows).transpose(0, 3, 2, 1, 4, 5)
    pieces = lax.all_to_all(
        pieces.reshape(8, 4 * share, rows), ("y", "core"), 0, 0, tiled=True
    )

    half = full.reshape(4, 2, 2, 2, share, cols)
    half = lax.dynamic_slice(half, (at["x"], 0, 0, 0, 0, z0 * rows), (1, 2, 2, 2, share, rows))
    half = half[0].transpose(1, 2, 0, 3, 4).reshape(8 * share, rows)
    normed = lax.ppermute(half, ROW + COL, row_block_pairs())
    other_normed = lax.ppermute(normed, "core", [(0, 1), (1, 0)])

    pieces = pieces.reshape(8, 2, 2 * share, rows)
    theirs = lax.dynamic_index_in_dim(pieces, 1 - zh, 1, keepdims=False).sum(0)
    mine = lax.dynamic_index_in_dim(pieces, zh, 1, keepdims=False).sum(0)
    arrived = lax.ppermute(theirs, "zh", [(0, 1), (1, 0)])
    kept = (mine + arrived) * keep_rows[None, :]

    first, second = product(kept, normed), product(kept, other_normed)
    ahead = (y % 2) ^ core
    term = jnp.concatenate(
        [jnp.where(ahead == 0, first, second), jnp.where(ahead == 0, second, first)], axis=1
    )
    term = copies(term, 8, ("x", "z0")).reshape(8, 2 * share, W).sum(0)
    term = copies(term, 4, ("zq", "zm")).reshape(4, 2 * share, W).sum(0)
    return (-kept).T, diag_inv + term.T


def solution(mesh):
    fine = Mesh(mesh.devices.reshape(SIZES), ROW + COL)
    placed = (P(ROW, COL), P(ROW, COL), P(), P(COL, ROW), P(None, COL))
    return jax.shard_map(
        body,
        mesh=fine,
        in_specs=placed,
        out_specs=(P(ROW, COL), P(None, COL)),
        check_vma=False,
    )
```

time: 138 us -> 125 us (0.906)
  the two profiles are of different devices: /device:TPU:6 before, /device:TPU:24 now
where the time goes in v4:
time: 125 us; the launch traced here: 124 us
  blocking collectives  55.5 us (44%)
  waiting for transfers between devices  40.1 us (32%)
  starting transfers between devices  21.1 us (17%)
  local copies, waits for them, and re-layouts  3.66 us (3%)
  matrix products  1.9 us (2%)
  other arithmetic  1.34 us (1%)
    all_to_all x3, blocking collectives, copies(): lax.all_to_all(jnp.broadcast_to(block[None], (count,) + block.shape), axe...  55.5 us
    all_to_all x1, waiting for transfers between devices, copies(): lax.all_to_all(jnp.broadcast_to(block[None], (count,) + block.shape), axe...  20.9 us
    ppermute x1, waiting for transfers between devices, body(): arrived = lax.ppermute(theirs, 'zh', [(0, 1), (1, 0)])  9.64 us
    all_to_all x1, waiting for transfers between devices, body(): lax.all_to_all(pieces.reshape(8, 4 * share, rows), ('y', 'core'), 0, 0, t...  9.59 us
    ppermute x1, starting transfers between devices, body(): arrived = lax.ppermute(theirs, 'zh', [(0, 1), (1, 0)])  6.92 us
    all_to_all x1, starting transfers between devices, copies(): lax.all_to_all(jnp.broadcast_to(block[None], (count,) + block.shape), axe...  5.17 us
    all_to_all x1, starting transfers between devices, body(): lax.all_to_all(pieces.reshape(8, 4 * share, rows), ('y', 'core'), 0, 0, t...  4.69 us
  transfers between devices with their start and end apart: 5, of which 3 were waited for; matrix products, arithmetic and copies ran while one was open for 1% of the time, Pallas kernels for 0%

profile of v4, /device:TPU:24, one launch (start us, length us, event | category | flops | bytes accessed | tf_op | source)
XLA Modules:
  0.0 124.4 jit_solution(10719516108491421561)
XLA Ops:
  0.6 0.8 broadcast_in_dim.14
  1.4 25.2 %all_to_all.25 = f32[4,16,768]{2,1,0:T(8,128)S(1)} all-to-all(f32[4,16,768]{2,1,0:T(8,128)S(1)} %broadcast_in_dim.14), channel_id=1, replica_groups=mesh['x'=4,'zq'=2,'zm'=2,'z0'=2,'y'=4,'zh'=2,'core'=2] {'zq','zm'}, dimensions={0} | all-to-all | bytes 393216 | tf_op jit(solution)/shard_map/all_to_all | solution.py:41
  26.7 1.3 %broadcast_in_dim.16 = f32[8,64,768]{2,1,0:T(8,128)} broadcast(f32[64,768]{1,0:T(8,128)S(1)} %bitcast.47), dimensions={1,2} | broadcast | bytes 1769472 | tf_op jit(solution)/shard_map/broadcast_in_dim | solution.py:41
  28.0 0.0 copy-start.2
  28.0 5.2 %all-to-all-start.1 = ((f32[8,64,768]{2,1,0:T(8,128)}), f32[8,64,768]{2,1,0:T(8,128)S(1)}, u32[]{:S(2)}, u32[]{:S(2)}) async-start(f32[8,64,768]{2,1,0:T(8,128)} %broadcast_in_dim.16), calls=%async_computation.1 | async-start | bytes 3145728 | tf_op jit(solution)/shard_map/all_to_all | solution.py:41
  33.1 0.0 copy-start
  33.2 0.0 copy-done.3
  33.2 0.1 fusion.9
  33.3 0.1 broadcast_bitcast_fusion
  33.4 0.0 copy-done.2
  33.4 20.9 %all-to-all-done.1 = f32[8,64,768]{2,1,0:T(8,128)S(1)} async-done(((f32[8,64,768]{2,1,0:T(8,128)}), f32[8,64,768]{2,1,0:T(8,128)S(1)}, u32[]{:S(2)}, u32[]{:S(2)}) %all-to-all-start.1) | async-done | bytes 1572896 | tf_op jit(solution)/shard_map/all_to_all | solution.py:41
  54.2 0.2 mul.69
  54.4 0.0 copy-done
  54.4 1.5 %fusion.2 = f32[4,2,2,2,16,384]{5,4,1,2,3,0:T(8,128)S(1)} fusion(f32[4,2,2,2,16,768]{5,4,3,2,1,0:T(8,128)S(1)} %bitcast.43, f32[384,768]{1,0:T(8,128)S(1)} %copy-done, f32[48,8,6,128]{3,2,1,0:T(8,128)S(1)} %bitcast.45, f32[4,768]{1,0:T(4,128)S(1)} %mul.66), kind=kOutput, calls=%fused_computation.2 | convolution fusion | flops 906657792 | bytes 4730880 | tf_op jit(solution)/shard_map/dot_general | solution.py:35
  55.9 1.0 copy.9
  56.9 4.7 %all-to-all-start.2 = ((f32[8,64,384]{2,1,0:T(8,128)}), f32[8,64,384]{2,1,0:T(8,128)S(1)}, u32[]{:S(2)}, u32[]{:S(2)}) async-start(f32[8,64,384]{2,1,0:T(8,128)} %bitcast.7), calls=%async_computation.2 | async-start | bytes 1572864 | tf_op jit(solution)/shard_map/all_to_all | solution.py:68
  61.6 0.1 constant_dynamic-slice_fusion.1
  61.7 2.4 %collective-permute-start.1 = (f32[128,384]{1,0:T(8,128)S(1)}, f32[128,384]{1,0:T(8,128)S(1)}, u32[]{:S(2)}, u32[]{:S(2)}) collective-permute-start(f32[128,384]{1,0:T(8,128)S(1)} %bitcast.48), channel_id=1, source_target_pairs={{0,0},{160,1},{64,2},{224,3},{128,4},{32,5},{192,6},{96,7},{256,8}... | collective-permute-start | bytes 589832 | tf_op jit(solution)/shard_map/ppermute | solution.py:75
  64.1 9.6 %all-to-all-done.2 = f32[8,64,384]{2,1,0:T(8,128)S(1)} async-done(((f32[8,64,384]{2,1,0:T(8,128)}), f32[8,64,384]{2,1,0:T(8,128)S(1)}, u32[]{:S(2)}, u32[]{:S(2)}) %all-to-all-start.2) | async-done | bytes 786464 | tf_op jit(solution)/shard_map/all_to_all | solution.py:68
  73.7 6.9 %collective-permute-start = (f32[32,384]{1,0:T(8,128)S(1)}, f32[32,384]{1,0:T(8,128)S(1)}, u32[]{:S(2)}, u32[]{:S(2)}) collective-permute-start(f32[32,384]{1,0:T(8,128)S(1)} %get-tuple-element.2), channel_id=1, source_target_pairs={{0,2},{2,0},{1,3},{3,1},{4,6},{6,4},{5,7},{7,5},{8,10},{10,8},{9,1... | collective-permute-start | bytes 147464 | tf_op jit(solution)/shard_map/ppermute | solution.py:81
  80.6 0.1 broadcast_bitcast_fusion.1
  80.7 0.0 collective-permute-done.1
  80.7 1.9 %collective-permute-start.2 = (f32[128,384]{1,0:T(8,128)S(1)}, f32[128,384]{1,0:T(8,128)S(1)}, u32[]{:S(2)}, u32[]{:S(2)}) collective-permute-start(f32[128,384]{1,0:T(8,128)S(1)} %collective-permute-done.1), channel_id=1, source_target_pairs={{0,1},{1,0},{2,3},{3,2},{4,5},{5,4},{6,7},{7,6},{8,9},{9,8},{10,11... | collective-permute-start | bytes 589832 | tf_op jit(solution)/shard_map/ppermute | solution.py:76
  82.6 9.6 %collective-permute-done = f32[32,384]{1,0:T(8,128)S(1)} collective-permute-done((f32[32,384]{1,0:T(8,128)S(1)}, f32[32,384]{1,0:T(8,128)S(1)}, u32[]{:S(2)}, u32[]{:S(2)}) %collective-permute-start) | collective-permute-done | bytes 49184 | tf_op jit(solution)/shard_map/ppermute | solution.py:81
  92.3 0.6 negate_bitcast_fusion
  92.9 0.2 fusion.11
  93.1 0.0 collective-permute-done.2
  93.1 0.2 broadcast_select_fusion.1
  93.4 13.2 %all_to_all.26 = f32[8,32,256]{2,1,0:T(8,128)S(1)} all-to-all(f32[8,32,256]{2,1,0:T(8,128)S(1)} %broadcast_in_dim.37), channel_id=1, replica_groups=mesh['x'=4,'zq'=2,'zm'=2,'z0'=2,'y'=4,'zh'=2,'core'=2] {'x','z0'}, dimensions={0} | all-to-all | bytes 524288 | tf_op jit(solution)/shard_map/all_to_all | solution.py:41
  106.6 17.1 %all_to_all.27 = f32[4,32,256]{2,1,0:T(8,128)S(1)} all-to-all(f32[4,32,256]{2,1,0:T(8,128)S(1)} %broadcast_in_dim.38), channel_id=1, replica_groups=mesh['x'=4,'zq'=2,'zm'=2,'z0'=2,'y'=4,'zh'=2,'core'=2] {'zq','zm'}, dimensions={0} | all-to-all | bytes 262144 | tf_op jit(solution)/shard_map/all_to_all | solution.py:41
  123.7 0.0 copy-done.1
  123.8 0.6 bitcast_add_fusion
  (16 shorter events, 0.2 us)
Async XLA Ops:
  28.0 5.2 %copy-start.3 = (s32[96,2]{0,1:T(2,128)S(1)}, s32[96,2]{0,1:T(2,128)}, u32[]{:S(2)}) copy-start(s32[96,2]{0,1:T(2,128)} %param.7) | copy-start | bytes 2308
  28.0 5.4 %copy-start.2 = (s32[3,6]{1,0:T(4,128)S(1)}, s32[3,6]{1,0:T(4,128)}, u32[]{:S(2)}) copy-start(s32[3,6]{1,0:T(4,128)} %param.6) | copy-start | bytes 220
  28.0 26.3 %all-to-all-start.1 = ((f32[8,64,768]{2,1,0:T(8,128)}), f32[8,64,768]{2,1,0:T(8,128)S(1)}, u32[]{:S(2)}, u32[]{:S(2)}) async-start(f32[8,64,768]{2,1,0:T(8,128)} %broadcast_in_dim.16), calls=%async_computation.1 | async-start | bytes 3145728 | tf_op jit(solution)/shard_map/all_to_all | solution.py:41
  33.1 21.3 %copy-start = (f32[384,768]{1,0:T(8,128)S(1)}, f32[384,768]{1,0:T(8,128)}, u32[]{:S(2)}) copy-start(f32[384,768]{1,0:T(8,128)} %param.5) | copy-start | bytes 3538948
  56.9 16.8 %all-to-all-start.2 = ((f32[8,64,384]{2,1,0:T(8,128)}), f32[8,64,384]{2,1,0:T(8,128)S(1)}, u32[]{:S(2)}, u32[]{:S(2)}) async-start(f32[8,64,384]{2,1,0:T(8,128)} %bitcast.7), calls=%async_computation.2 | async-start | bytes 1572864 | tf_op jit(solution)/shard_map/all_to_all | solution.py:68
  61.7 19.0 %collective-permute-start.1 = (f32[128,384]{1,0:T(8,128)S(1)}, f32[128,384]{1,0:T(8,128)S(1)}, u32[]{:S(2)}, u32[]{:S(2)}) collective-permute-start(f32[128,384]{1,0:T(8,128)S(1)} %bitcast.48), channel_id=1, source_target_pairs={{0,0},{160,1},{64,2},{224,3},{128,4},{32,5},{192,6},{96,7},{256,8}... | collective-permute-start | bytes 589832 | tf_op jit(solution)/shard_map/ppermute | solution.py:75
  73.7 50.1 %copy-start.1 = (f32[256,32]{0,1:T(8,128)S(1)}, f32[256,32]{0,1:T(8,128)}, u32[]{:S(2)}) copy-start(f32[256,32]{0,1:T(8,128)} %param.9) | copy-start | bytes 98308
  73.7 18.6 %collective-permute-start = (f32[32,384]{1,0:T(8,128)S(1)}, f32[32,384]{1,0:T(8,128)S(1)}, u32[]{:S(2)}, u32[]{:S(2)}) collective-permute-start(f32[32,384]{1,0:T(8,128)S(1)} %get-tuple-element.2), channel_id=1, source_target_pairs={{0,2},{2,0},{1,3},{3,1},{4,6},{6,4},{5,7},{7,5},{8,10},{10,8},{9,1... | collective-permute-start | bytes 147464 | tf_op jit(solution)/shard_map/ppermute | solution.py:81
  80.7 12.4 %collective-permute-start.2 = (f32[128,384]{1,0:T(8,128)S(1)}, f32[128,384]{1,0:T(8,128)S(1)}, u32[]{:S(2)}, u32[]{:S(2)}) collective-permute-start(f32[128,384]{1,0:T(8,128)S(1)} %collective-permute-done.1), channel_id=1, source_target_pairs={{0,1},{1,0},{2,3},{3,2},{4,5},{5,4},{6,7},{7,6},{8,9},{9,8},{10,11... | collective-permute-start | bytes 589832 | tf_op jit(solution)/shard_map/ppermute | solution.py:76

commit v5 on v4

--- a/solution.py
+++ b/solution.py
@@ -62,12 +62,17 @@
 
     four = copies(panel.T, 4, ("zq", "zm"))
     full = copies(four.reshape(4 * share, cols), 8, ("x", "z0"))
-    kept_cols = full.reshape(2, 16 * share, cols) * keep_cols[:, None, :]
-    partial_sum = product(kept_cols.reshape(32 * share, cols), masked)
-    pieces = partial_sum.reshape(4, 2, 2, 2, share, rows).transpose(0, 3, 2, 1, 4, 5)
-    pieces = lax.all_to_all(
-        pieces.reshape(8, 4 * share, rows), ("y", "core"), 0, 0, tiled=True
-    )
+    sides = full.reshape(8, 2, 2 * share, cols)
+
+    def reduced(side):
+        block = lax.dynamic_index_in_dim(sides, side, 1, keepdims=False)
+        block = block.reshape(2, 8 * share, cols) * keep_cols[:, None, :]
+        partial_sum = product(block.reshape(16 * share, cols), masked)
+        pieces = partial_sum.reshape(4, 2, 2, share, rows).transpose(0, 2, 1, 3, 4)
+        pieces = lax.all_to_all(pieces.reshape(8, 2 * share, rows), ("y", "core"), 0, 0, tiled=True)
+        return pieces
+
+    theirs, mine = reduced(1 - zh), reduced(zh)
 
     half = full.reshape(4, 2, 2, 2, share, cols)
     half = lax.dynamic_slice(half, (at["x"], 0, 0, 0, 0, z0 * rows), (1, 2, 2, 2, share, rows))
@@ -75,11 +80,9 @@
     normed = lax.ppermute(half, ROW + COL, row_block_pairs())
     other_normed = lax.ppermute(normed, "core", [(0, 1), (1, 0)])
 
-    pieces = pieces.reshape(8, 2, 2 * share, rows)
-    theirs = lax.dynamic_index_in_dim(pieces, 1 - zh, 1, keepdims=False).sum(0)
-    mine = lax.dynamic_index_in_dim(pieces, zh, 1, keepdims=False).sum(0)
+    theirs = theirs.sum(0)
     arrived = lax.ppermute(theirs, "zh", [(0, 1), (1, 0)])
-    kept = (mine + arrived) * keep_rows[None, :]
+    kept = (mine.sum(0) + arrived) * keep_rows[None, :]
 
     first, second = product(kept, normed), product(kept, other_normed)
     ahead = (y % 2) ^ core

time: 125 us -> 139 us (1.11)
  the two profiles are of different devices: /device:TPU:24 before, /device:TPU:16 now
where the time goes in v5:
time: 139 us
  blocking collectives  68.9 us (50%)
  starting transfers between devices  30.6 us (22%)
  waiting for transfers between devices  26.3 us (19%)
  local copies, waits for them, and re-layouts  6.93 us (5%)
  matrix products  3.79 us (3%)
    all_to_all x3, blocking collectives, copies(): lax.all_to_all(jnp.broadcast_to(block[None], (count,) + block.shape), axe...  68.9 us
    all_to_all x1, waiting for transfers between devices, copies(): lax.all_to_all(jnp.broadcast_to(block[None], (count,) + block.shape), axe...  20.9 us
    all_to_all x2, starting transfers between devices, reduced(): lax.all_to_all(pieces.reshape(8, 2 * share, rows), ('y', 'core'), 0, 0, t...  11.3 us
    ppermute x1, starting transfers between devices, body(): arrived = lax.ppermute(theirs, 'zh', [(0, 1), (1, 0)])  7.99 us
    all_to_all x1, starting transfers between devices, copies(): lax.all_to_all(jnp.broadcast_to(block[None], (count,) + block.shape), axe...  5.17 us
    ppermute x1, starting transfers between devices, body(): other_normed = lax.ppermute(normed, 'core', [(0, 1), (1, 0)])  3.84 us
    dot_general x4, matrix products, product(): lax.dot_general(left, right, (((1,), (1,)), ((), ())), precision=CLOSE, p...  3.79 us
    ppermute x1, waiting for transfers between devices, body(): normed = lax.ppermute(half, ROW + COL, row_block_pairs())  3.34 us
  transfers between devices with their start and end apart: 6, of which 5 were waited for; matrix products, arithmetic and copies ran while one was open for 4% of the time, Pallas kernels for 0%

profile of v5, /device:TPU:16, one launch (start us, length us, event | category | flops | bytes accessed | tf_op | source)
XLA Modules:
  0.0 138.7 jit_solution(8771415154204007449)
XLA Ops:
  0.6 0.8 broadcast_in_dim.14
  1.4 25.2 %all_to_all.30 = f32[4,16,768]{2,1,0:T(8,128)S(1)} all-to-all(f32[4,16,768]{2,1,0:T(8,128)S(1)} %broadcast_in_dim.14), channel_id=1, replica_groups=mesh['x'=4,'zq'=2,'zm'=2,'z0'=2,'y'=4,'zh'=2,'core'=2] {'zq','zm'}, dimensions={0} | all-to-all | bytes 393216 | tf_op jit(solution)/shard_map/all_to_all | solution.py:41
  26.7 1.3 broadcast_in_dim.16
  28.0 5.2 %all-to-all-start.1 = ((f32[8,64,768]{2,1,0:T(8,128)}), f32[8,64,768]{2,1,0:T(8,128)S(1)}, u32[]{:S(2)}, u32[]{:S(2)}) async-start(f32[8,64,768]{2,1,0:T(8,128)} %broadcast_in_dim.16), calls=%async_computation.1 | async-start | bytes 3145728 | tf_op jit(solution)/shard_map/all_to_all | solution.py:41
  33.2 0.1 fusion.7
  33.2 0.1 broadcast_bitcast_fusion
  33.4 20.9 %all-to-all-done.1 = f32[8,64,768]{2,1,0:T(8,128)S(1)} async-done(((f32[8,64,768]{2,1,0:T(8,128)}), f32[8,64,768]{2,1,0:T(8,128)S(1)}, u32[]{:S(2)}, u32[]{:S(2)}) %all-to-all-start.1) | async-done | bytes 1572896 | tf_op jit(solution)/shard_map/all_to_all | solution.py:41
  54.2 1.0 constant_dynamic-slice_fusion.2
  55.3 0.2 mul.77
  55.4 1.1 copy-done
  56.5 0.9 convolution_bitcast_fusion
  57.5 0.8 copy.11
  58.3 4.8 %all-to-all-start.3 = ((f32[8,32,384]{2,1,0:T(8,128)}), f32[8,32,384]{2,1,0:T(8,128)S(1)}, u32[]{:S(2)}, u32[]{:S(2)}) async-start(f32[8,32,384]{2,1,0:T(8,128)} %bitcast.56), calls=%async_computation.3 | async-start | bytes 786432 | tf_op jit(solution)/shard_map/all_to_all | solution.py:72
  63.1 0.6 constant_dynamic-slice_fusion.1
  63.7 2.4 %convolution_bitcast_fusion.1 = f32[4,2,2,16,384]{4,3,1,2,0:T(8,128)S(1)} fusion(f32[4,2,2,16,768]{4,3,2,1,0:T(8,128)} %bitcast.54, f32[4,768]{1,0:T(4,128)S(1)} %mul.74, f32[384,768]{1,0:T(8,128)} %param.5, f32[48,8,6,128]{3,2,1,0:T(8,128)S(1)} %bitcast.51), kind=kOutput, calls=%fused_computation.1 | convolution fusion | flops 453476352 | bytes 3551232 | tf_op jit(solution)/shard_map/dot_general | solution.py:35
  66.1 0.0 copy-start.2
  66.2 0.8 copy.10
  66.9 1.9 %all-to-all-done.3 = f32[8,32,384]{2,1,0:T(8,128)S(1)} async-done(((f32[8,32,384]{2,1,0:T(8,128)}), f32[8,32,384]{2,1,0:T(8,128)S(1)}, u32[]{:S(2)}, u32[]{:S(2)}) %all-to-all-start.3) | async-done | bytes 393248 | tf_op jit(solution)/shard_map/all_to_all | solution.py:72
  68.8 6.5 %all-to-all-start.2 = ((f32[8,32,384]{2,1,0:T(8,128)}), f32[8,32,384]{2,1,0:T(8,128)S(1)}, u32[]{:S(2)}, u32[]{:S(2)}) async-start(f32[8,32,384]{2,1,0:T(8,128)} %bitcast.8), calls=%async_computation.2 | async-start | bytes 786432 | tf_op jit(solution)/shard_map/all_to_all | solution.py:72
  75.4 2.3 %collective-permute-start.1 = (f32[128,384]{1,0:T(8,128)S(1)}, f32[128,384]{1,0:T(8,128)S(1)}, u32[]{:S(2)}, u32[]{:S(2)}) collective-permute-start(f32[128,384]{1,0:T(8,128)S(1)} %bitcast.58), channel_id=1, source_target_pairs={{0,0},{160,1},{64,2},{224,3},{128,4},{32,5},{192,6},{96,7},{256,8}... | collective-permute-start | bytes 589832 | tf_op jit(solution)/shard_map/ppermute | solution.py:80
  77.8 8.0 %collective-permute-start = (f32[32,384]{1,0:T(8,128)S(1)}, f32[32,384]{1,0:T(8,128)S(1)}, u32[]{:S(2)}, u32[]{:S(2)}) collective-permute-start(f32[32,384]{1,0:T(8,128)S(1)} %reduce_sum.37), channel_id=1, source_target_pairs={{0,2},{2,0},{1,3},{3,1},{4,6},{6,4},{5,7},{7,5},{8,10},{10,8},{9,1... | collective-permute-start | bytes 147464 | tf_op jit(solution)/shard_map/ppermute | solution.py:84
  85.7 0.1 broadcast_bitcast_fusion.1
  85.8 3.3 %collective-permute-done.1 = f32[128,384]{1,0:T(8,128)S(1)} collective-permute-done((f32[128,384]{1,0:T(8,128)S(1)}, f32[128,384]{1,0:T(8,128)S(1)}, u32[]{:S(2)}, u32[]{:S(2)}) %collective-permute-start.1) | collective-permute-done | bytes 196640 | tf_op jit(solution)/shard_map/ppermute | solution.py:80
  89.2 3.8 %collective-permute-start.2 = (f32[128,384]{1,0:T(8,128)S(1)}, f32[128,384]{1,0:T(8,128)S(1)}, u32[]{:S(2)}, u32[]{:S(2)}) collective-permute-start(f32[128,384]{1,0:T(8,128)S(1)} %collective-permute-done.1), channel_id=1, source_target_pairs={{0,1},{1,0},{2,3},{3,2},{4,5},{5,4},{6,7},{7,6},{8,9},{9,8},{10,11... | collective-permute-start | bytes 589832 | tf_op jit(solution)/shard_map/ppermute | solution.py:81
  93.0 0.1 collective-permute-done
  93.1 0.6 negate_bitcast_fusion
  93.8 0.2 fusion.9
  94.0 0.1 collective-permute-done.2
  94.1 0.2 broadcast_select_fusion.1
  94.3 19.1 %all_to_all.31 = f32[8,32,256]{2,1,0:T(8,128)S(1)} all-to-all(f32[8,32,256]{2,1,0:T(8,128)S(1)} %broadcast_in_dim.37), channel_id=1, replica_groups=mesh['x'=4,'zq'=2,'zm'=2,'z0'=2,'y'=4,'zh'=2,'core'=2] {'x','z0'}, dimensions={0} | all-to-all | bytes 524288 | tf_op jit(solution)/shard_map/all_to_all | solution.py:41
  113.5 24.6 %all_to_all.32 = f32[4,32,256]{2,1,0:T(8,128)S(1)} all-to-all(f32[4,32,256]{2,1,0:T(8,128)S(1)} %broadcast_in_dim.38), channel_id=1, replica_groups=mesh['x'=4,'zq'=2,'zm'=2,'z0'=2,'y'=4,'zh'=2,'core'=2] {'zq','zm'}, dimensions={0} | all-to-all | bytes 262144 | tf_op jit(solution)/shard_map/all_to_all | solution.py:41
  138.1 0.6 bitcast_add_fusion
  (24 shorter events, 0.2 us)
Async XLA Ops:
  27.9 5.2 %copy-start.4 = (s32[96,2]{0,1:T(2,128)S(1)}, s32[96,2]{0,1:T(2,128)}, u32[]{:S(2)}) copy-start(s32[96,2]{0,1:T(2,128)} %param.7) | copy-start | bytes 2308
  27.9 5.2 %copy-start.3 = (s32[3,6]{1,0:T(4,128)S(1)}, s32[3,6]{1,0:T(4,128)}, u32[]{:S(2)}) copy-start(s32[3,6]{1,0:T(4,128)} %param.6) | copy-start | bytes 220
  28.0 26.3 %all-to-all-start.1 = ((f32[8,64,768]{2,1,0:T(8,128)}), f32[8,64,768]{2,1,0:T(8,128)S(1)}, u32[]{:S(2)}, u32[]{:S(2)}) async-start(f32[8,64,768]{2,1,0:T(8,128)} %broadcast_in_dim.16), calls=%async_computation.1 | async-start | bytes 3145728 | tf_op jit(solution)/shard_map/all_to_all | solution.py:41
  55.3 1.3 copy-start
  58.3 10.6 %all-to-all-start.3 = ((f32[8,32,384]{2,1,0:T(8,128)}), f32[8,32,384]{2,1,0:T(8,128)S(1)}, u32[]{:S(2)}, u32[]{:S(2)}) async-start(f32[8,32,384]{2,1,0:T(8,128)} %bitcast.56), calls=%async_computation.3 | async-start | bytes 786432 | tf_op jit(solution)/shard_map/all_to_all | solution.py:72
  66.1 9.2 %copy-start.2 = (f32[3,2]{0,1:T(2,128)S(1)}, f32[3,2]{0,1:T(2,128)}, u32[]{:S(2)}) copy-start(f32[3,2]{0,1:T(2,128)} %constant_dynamic-slice_fusion.1) | copy-start | bytes 76
  68.8 24.2 %all-to-all-start.2 = ((f32[8,32,384]{2,1,0:T(8,128)}), f32[8,32,384]{2,1,0:T(8,128)S(1)}, u32[]{:S(2)}, u32[]{:S(2)}) async-start(f32[8,32,384]{2,1,0:T(8,128)} %bitcast.8), calls=%async_computation.2 | async-start | bytes 786432 | tf_op jit(solution)/shard_map/all_to_all | solution.py:72
  75.4 13.7 %collective-permute-start.1 = (f32[128,384]{1,0:T(8,128)S(1)}, f32[128,384]{1,0:T(8,128)S(1)}, u32[]{:S(2)}, u32[]{:S(2)}) collective-permute-start(f32[128,384]{1,0:T(8,128)S(1)} %bitcast.58), channel_id=1, source_target_pairs={{0,0},{160,1},{64,2},{224,3},{128,4},{32,5},{192,6},{96,7},{256,8}... | collective-permute-start | bytes 589832 | tf_op jit(solution)/shard_map/ppermute | solution.py:80
  77.8 15.4 %collective-permute-start = (f32[32,384]{1,0:T(8,128)S(1)}, f32[32,384]{1,0:T(8,128)S(1)}, u32[]{:S(2)}, u32[]{:S(2)}) collective-permute-start(f32[32,384]{1,0:T(8,128)S(1)} %reduce_sum.37), channel_id=1, source_target_pairs={{0,2},{2,0},{1,3},{3,1},{4,6},{6,4},{5,7},{7,5},{8,10},{10,8},{9,1... | collective-permute-start | bytes 147464 | tf_op jit(solution)/shard_map/ppermute | solution.py:84
  89.2 4.9 %collective-permute-start.2 = (f32[128,384]{1,0:T(8,128)S(1)}, f32[128,384]{1,0:T(8,128)S(1)}, u32[]{:S(2)}, u32[]{:S(2)}) collective-permute-start(f32[128,384]{1,0:T(8,128)S(1)} %collective-permute-done.1), channel_id=1, source_target_pairs={{0,1},{1,0},{2,3},{3,2},{4,5},{5,4},{6,7},{7,6},{8,9},{9,8},{10,11... | collective-permute-start | bytes 589832 | tf_op jit(solution)/shard_map/ppermute | solution.py:81
  93.8 44.3 %copy-start.1 = (f32[256,32]{0,1:T(8,128)S(1)}, f32[256,32]{0,1:T(8,128)}, u32[]{:S(2)}) copy-start(f32[256,32]{0,1:T(8,128)} %param.9) | copy-start | bytes 98308

commit v6 on v4

v6 whole, which is shorter than its diff:
```python
import jax
import jax.numpy as jnp
from jax import lax
from jax.experimental import pallas as pl
from jax.experimental.pallas import tpu as pltpu
from jax.sharding import Mesh, PartitionSpec as P


W = 256
BS = 128
ROW = ("x", "zq", "zm", "z0")
COL = ("y", "zh", "core")
SIZES = (4, 2, 2, 2, 4, 2, 2)
CLOSE = lax.Precision.HIGH
IN_VMEM = pl.BlockSpec(memory_space=pltpu.VMEM)
IN_HBM = pl.BlockSpec(memory_space=pltpu.HBM)
IN_SMEM = pl.BlockSpec(memory_space=pltpu.SMEM)


def pairs_to(source_of):
    pairs = []
    for target in range(512):
        rest, place = target, []
        for size in reversed(SIZES):
            place.insert(0, rest % size)
            rest //= size
        source = 0
        for size, part in zip(SIZES, source_of(*place)):
            source = source * size + part
        pairs.append((source, target))
    return pairs


def send(values, source_of):
    return lax.ppermute(values, ROW + COL, pairs_to(source_of))


def swapped(bit, first, second):
    return [jnp.where(bit == 0, first, second), jnp.where(bit == 0, second, first)]


def parts_of(values):
    high = values.astype(jnp.bfloat16)
    return high, (values - high.astype(jnp.float32)).astype(jnp.bfloat16)


def mask_blocks(pattern_ref, ancestor_ref, out_ref):
    for a in range(pattern_ref.shape[0]):
        for b in range(pattern_ref.shape[1]):
            place = (pl.ds(a * BS, BS), pl.ds(b * BS, BS))
            out_ref[place] = ancestor_ref[place] * pattern_ref[a, b].astype(jnp.float32)


def split_blocks(own_ref, other_ref, high_ref, low_ref):
    for slot, ref in enumerate((own_ref, other_ref)):
        for b in range(ref.shape[1] // BS):
            here = pl.ds(b * BS, BS)
            high_ref[slot, here, :], low_ref[slot, here, :] = parts_of(ref[:, here].T)


def block_product(
    turn_ref, full_hbm, keep_ref, high_hbm, low_hbm, out_ref, full_ref, high_ref, low_ref, sems
):
    turn = turn_ref[0]
    fetched = [pltpu.make_async_copy(full_hbm, full_ref, sems.at[0])]
    for j in range(2):
        for n, (hbm, ref) in enumerate(((high_hbm, high_ref), (low_hbm, low_ref))):
            fetched.append(pltpu.make_async_copy(hbm.at[turn ^ j], ref.at[j], sems.at[1 + 2 * j + n]))
    for copy in fetched:
        copy.start()
    fetched[0].wait()
    total = 0.0
    for j in range(2):
        lines = []
        for x in range(4):
            for zq in range(2):
                for z0 in range(2):
                    block = full_ref[2 * x + z0, pl.ds((2 * zq + j) * 16, 16), :]
                    lines.append(block * keep_ref[pl.ds(2 * j + x // 2, 1), :])
        high, low = parts_of(jnp.concatenate(lines, axis=0))
        fetched[1 + 2 * j].wait()
        fetched[2 + 2 * j].wait()
        for left, right_ref in ((high, high_ref), (high, low_ref), (low, high_ref)):
            total += jnp.dot(left, right_ref[j], preferred_element_type=jnp.float32)
    out_ref[...] = total.reshape(out_ref.shape)


def kernel_call(body, out_shape, in_specs, out_specs, limit, flops, moved, scratch=()):
    return pl.pallas_call(
        body,
        out_shape=out_shape,
        in_specs=in_specs,
        out_specs=out_specs,
        scratch_shapes=scratch,
        compiler_params=pltpu.CompilerParams(vmem_limit_bytes=limit),
        cost_estimate=pl.CostEstimate(flops=flops, bytes_accessed=moved, transcendentals=0),
    )


def product(left, right):
    return lax.dot_general(
        left, right, (((1,), (1,)), ((), ())), precision=CLOSE, preferred_element_type=jnp.float32
    )


def copies(block, count, axes):
    return lax.all_to_all(jnp.broadcast_to(block[None], (count,) + block.shape), axes, 0, 0, tiled=True)


def body(ancestor, pattern, member, panel, diag_inv):
    at = {name: lax.axis_index(name) for name in ROW + COL}
    zq, zm, z0, y, zh, core = (at[name] for name in ("zq", "zm", "z0", "y", "zh", "core"))
    row = at["x"] * 8 + zq * 4 + zm * 2 + z0
    pair = y * 2 + zh
    row_blocks, col_blocks = pattern.shape
    rows, cols = ancestor.shape
    share = panel.shape[1]

    own = panel.T
    taken = [
        [
            send(own, lambda x, zq, zm, z0, y, zh, core: (x, zq ^ i, core, z0, y, zh, zm ^ j))
            for j in range(2)
        ]
        for i in range(2)
    ]
    part = jnp.stack([block for line in taken for block in line]).reshape(4 * share, cols)

    whole = jax.ShapeDtypeStruct((rows, cols), jnp.float32)
    masked = kernel_call(
        mask_blocks, whole, [IN_SMEM, IN_VMEM], IN_VMEM, 8 << 20, 10**6, 2 * 10**6
    )(pattern, ancestor)
    other_masked = lax.ppermute(masked, "core", [(0, 1), (1, 0)])
    split = jax.ShapeDtypeStruct((2, cols, rows), jnp.bfloat16)
    high, low = kernel_call(
        split_blocks,
        (split, split),
        [IN_VMEM, IN_VMEM],
        (IN_VMEM, IN_VMEM),
        16 << 20,
        10**6,
        5 * 10**6,
    )(masked, other_masked)

    flags = member.astype(jnp.float32)
    keep_rows = lax.dynamic_slice_in_dim(flags, row * row_blocks, row_blocks, 0)
    keep_rows = jnp.repeat(jnp.where(y // 2 == 0, keep_rows[:, 0], keep_rows[:, 1]), BS)
    both = lax.dynamic_slice_in_dim(flags, pair * 2 * col_blocks, 2 * col_blocks, 0)
    both = both.reshape(2, col_blocks, 2).transpose(0, 2, 1)
    keep_cols = jnp.repeat(jnp.stack(swapped(zm, both[0], both[1])).reshape(4, col_blocks), BS, axis=1)

    full = copies(part, 8, ("x", "z0"))

    wanted = jnp.stack(swapped(zq, taken[0][0], taken[1][0])).reshape(2 * share, cols)
    near = [
        send(
            lax.dynamic_slice_in_dim(wanted, (z0 ^ t) * rows, rows, 1),
            lambda x, zq, zm, z0, y, zh, core: (y, zh, zm, z0 ^ t, x, zq, core),
        ).reshape(2, share, rows)
        for t in range(2)
    ]
    pieces = kernel_call(
        block_product,
        jax.ShapeDtypeStruct((4, 4 * share, rows), jnp.float32),
        [IN_SMEM, IN_HBM, IN_VMEM, IN_HBM, IN_HBM],
        IN_VMEM,
        62000000,
        900 * 10**6,
        5 * 10**6,
        [
            pltpu.VMEM((8, 4 * share, cols), jnp.float32),
            pltpu.VMEM((2, cols, rows), jnp.bfloat16),
            pltpu.VMEM((2, cols, rows), jnp.bfloat16),
            pltpu.SemaphoreType.DMA((5,)),
        ],
    )((zm ^ core).reshape(1), full, keep_cols, high, low)
    pieces, *near = lax.optimization_barrier((pieces, *near))
    pieces = lax.all_to_all(pieces, "y", 0, 0, tiled=True).reshape(4, 2, 2 * share, rows)
    near = jnp.stack(swapped(z0, near[0], near[1]), axis=1).reshape(4 * share, rows)
    far = lax.ppermute(near, "y", [(i, i ^ 1) for i in range(4)])
    near = jnp.stack(swapped(y % 2, near, far)).reshape(8 * share, rows)
    far = lax.ppermute(near, "core", [(0, 1), (1, 0)])
    normed = jnp.stack(
        swapped(core, near.reshape(4, 2 * share, rows), far.reshape(4, 2 * share, rows)), axis=1
    ).reshape(W, rows)

    theirs = lax.dynamic_index_in_dim(pieces, 1 - (zh ^ zq), 1, keepdims=False).sum(0)
    mine = lax.dynamic_index_in_dim(pieces, zh ^ zq, 1, keepdims=False).sum(0)
    arrived = lax.ppermute(theirs, "zh", [(0, 1), (1, 0)])
    kept = (mine + arrived) * keep_rows[None, :]

    kept, inverse = lax.optimization_barrier((kept, -kept))
    term = product(kept, normed)
    term = copies(term, 8, ("x", "z0")).reshape(8, 2 * share, W).sum(0)
    term = copies(term, 4, ("zq", "zm")).reshape(4, 2 * share, W).sum(0)
    return inverse.T, diag_inv + term.T


def solution(mesh):
    fine = Mesh(mesh.devices.reshape(SIZES), ROW + COL)
    placed = (P(ROW, COL), P(ROW, COL), P(), P(COL, ROW), P(None, COL))
    return jax.shard_map(
        body,
        mesh=fine,
        in_specs=placed,
        out_specs=(P(ROW, COL), P(None, COL)),
        check_vma=False,
    )
```

time: 125 us -> 121 us (0.968)
  the two profiles are of different devices: /device:TPU:24 before, /device:TPU:6 now
where the time goes in v6:
time: 121 us; the launch traced here: 120 us
  starting transfers between devices  60.2 us (50%)
  blocking collectives  29.1 us (24%)
  waiting for transfers between devices  17.2 us (14%)
  Pallas kernels  6.21 us (5%)
  local copies, waits for them, and re-layouts  4.41 us (4%)
  other arithmetic  1.48 us (1%)
    all_to_all x2, blocking collectives, copies(): lax.all_to_all(jnp.broadcast_to(block[None], (count,) + block.shape), axe...  29.1 us
    ppermute x6, starting transfers between devices, send(): return lax.ppermute(values, ROW + COL, pairs_to(source_of))  27.2 us
    ppermute x1, starting transfers between devices, body(): arrived = lax.ppermute(theirs, 'zh', [(0, 1), (1, 0)])  15.7 us
    all_to_all x1, starting transfers between devices, copies(): lax.all_to_all(jnp.broadcast_to(block[None], (count,) + block.shape), axe...  5.97 us
    ppermute x6, waiting for transfers between devices, send(): return lax.ppermute(values, ROW + COL, pairs_to(source_of))  5.41 us
    all_to_all x1, waiting for transfers between devices, body(): lax.all_to_all(pieces, 'y', 0, 0, tiled=True).reshape(4, 2, 2 * share, rows)  5.33 us
    pallas_call x1, Pallas kernels, body(): kernel_call(block_product, jax.ShapeDtypeStruct((4, 4 * share, rows), jnp...  4.89 us
    all_to_all x1, waiting for transfers between devices, copies(): lax.all_to_all(jnp.broadcast_to(block[None], (count,) + block.shape), axe...  4.51 us
  transfers between devices with their start and end apart: 12, of which 5 were waited for; matrix products, arithmetic and copies ran while one was open for 1% of the time, Pallas kernels for 5%

profile of v6, /device:TPU:6, one launch (start us, length us, event | category | flops | bytes accessed | tf_op | source)
XLA Modules:
  0.0 119.8 jit_solution(1739433483061279661)
XLA Ops:
  0.6 11.8 %collective-permute-start.3 = (f32[16,768]{1,0:T(8,128)}, f32[16,768]{1,0:T(8,128)S(1)}, u32[]{:S(2)}, u32[]{:S(2)}) collective-permute-start(f32[16,768]{1,0:T(8,128)} %bitcast.71), channel_id=1, source_target_pairs={{65,0},{97,1},{67,2},{99,3},{69,4},{101,5},{71,6},{103,7},{73,8},{... | collective-permute-start | bytes 147464 | tf_op jit(solution)/shard_map/ppermute | solution.py:35
  12.4 1.9 %collective-permute-start.2 = (f32[16,768]{1,0:T(8,128)}, f32[16,768]{1,0:T(8,128)S(1)}, u32[]{:S(2)}, u32[]{:S(2)}) collective-permute-start(f32[16,768]{1,0:T(8,128)} %bitcast.72), channel_id=1, source_target_pairs={{64,0},{96,1},{66,2},{98,3},{68,4},{100,5},{70,6},{102,7},{72,8},{... | collective-permute-start | bytes 147464 | tf_op jit(solution)/shard_map/ppermute | solution.py:35
  14.4 1.9 %collective-permute-start.1 = (f32[16,768]{1,0:T(8,128)}, f32[16,768]{1,0:T(8,128)S(1)}, u32[]{:S(2)}, u32[]{:S(2)}) collective-permute-start(f32[16,768]{1,0:T(8,128)} %bitcast.73), channel_id=1, source_target_pairs={{1,0},{33,1},{3,2},{35,3},{5,4},{37,5},{7,6},{39,7},{9,8},{41,9},{... | collective-permute-start | bytes 147464 | tf_op jit(solution)/shard_map/ppermute | solution.py:35
  16.3 1.5 %collective-permute-start = (f32[16,768]{1,0:T(8,128)}, f32[16,768]{1,0:T(8,128)S(1)}, u32[]{:S(2)}, u32[]{:S(2)}) collective-permute-start(f32[16,768]{1,0:T(8,128)} %bitcast.74), channel_id=1, source_target_pairs={{0,0},{32,1},{2,2},{34,3},{4,4},{36,5},{6,6},{38,7},{8,8},{40,9},{... | collective-permute-start | bytes 147464 | tf_op jit(solution)/shard_map/ppermute | solution.py:35
  17.8 5.3 %collective-permute-done.2 = f32[16,768]{1,0:T(8,128)S(1)} collective-permute-done((f32[16,768]{1,0:T(8,128)}, f32[16,768]{1,0:T(8,128)S(1)}, u32[]{:S(2)}, u32[]{:S(2)}) %collective-permute-start.2) | collective-permute-done | bytes 49184 | tf_op jit(solution)/shard_map/ppermute | solution.py:35
  23.1 1.3 %broadcast_in_dim.26 = f32[8,64,768]{2,1,0:T(8,128)} broadcast(f32[64,768]{1,0:T(8,128)S(1)} %bitcast.55), dimensions={1,2} | broadcast | bytes 1769472 | tf_op jit(solution)/shard_map/broadcast_in_dim | solution.py:107
  24.4 6.0 %all-to-all-start = ((f32[8,64,768]{2,1,0:T(8,128)}), f32[8,64,768]{2,1,0:T(8,128)}, u32[]{:S(2)}, u32[]{:S(2)}) async-start(f32[8,64,768]{2,1,0:T(8,128)} %broadcast_in_dim.26), calls=%async_computation | async-start | bytes 3145728 | tf_op jit(solution)/shard_map/all_to_all | solution.py:107
  30.4 0.6 shard_map.68.own_ref
  31.0 1.9 %collective-permute-start.4 = (f32[384,768]{1,0:T(8,128)S(1)}, f32[384,768]{1,0:T(8,128)S(1)}, u32[]{:S(2)}, u32[]{:S(2)}) collective-permute-start(f32[384,768]{1,0:T(8,128)S(1)} %shard_map.68.own_ref), channel_id=1, source_target_pairs={{0,1},{1,0},{2,3},{3,2},{4,5},{5,4},{6,7},{7,6},{8,9},{9,8},{10,11... | collective-permute-start | bytes 3538952 | tf_op jit(solution)/shard_map/ppermute | solution.py:133
  33.0 0.1 constant_dynamic-slice_fusion.3
  33.1 0.1 reshape.81
  33.2 0.6 copy.20
  33.9 0.1 constant_dynamic-slice_fusion
  34.0 5.8 %collective-permute-start.6 = (f32[32,384]{1,0:T(8,128)S(1)}, f32[32,384]{1,0:T(8,128)S(1)}, u32[]{:S(2)}, u32[]{:S(2)}) collective-permute-start(f32[32,384]{1,0:T(8,128)S(1)} %get-tuple-element.26), channel_id=1, source_target_pairs={{16,0},{17,1},{80,2},{81,3},{144,4},{145,5},{208,6},{209,7},{272,8... | collective-permute-start | bytes 147464 | tf_op jit(solution)/shard_map/ppermute | solution.py:35
  39.8 4.2 %collective-permute-start.5 = (f32[32,384]{1,0:T(8,128)S(1)}, f32[32,384]{1,0:T(8,128)S(1)}, u32[]{:S(2)}, u32[]{:S(2)}) collective-permute-start(f32[32,384]{1,0:T(8,128)S(1)} %get-tuple-element.27), channel_id=1, source_target_pairs={{0,0},{1,1},{64,2},{65,3},{128,4},{129,5},{192,6},{193,7},{256,8},... | collective-permute-start | bytes 147464 | tf_op jit(solution)/shard_map/ppermute | solution.py:35
  44.1 0.7 shard_map.69
  44.8 1.0 copy-done.1
  45.8 1.1 copy-done.2
  46.8 4.5 %all-to-all-done.full_hbm = f32[8,64,768]{2,1,0:T(8,128)} async-done(((f32[8,64,768]{2,1,0:T(8,128)}), f32[8,64,768]{2,1,0:T(8,128)}, u32[]{:S(2)}, u32[]{:S(2)}) %all-to-all-start) | async-done | bytes 1572896 | tf_op jit(solution)/shard_map/all_to_all | solution.py:107
  51.4 4.9 %shard_map.70 = f32[4,64,384]{2,1,0:T(8,128)} custom-call(s32[1]{0:T(128)} %bitcast.turn_ref, f32[8,64,768]{2,1,0:T(8,128)} %all-to-all-done.full_hbm, f32[4,768]{1,0:T(4,128)} %bitcast.68, bf16[2,768,384]{2,1,0:T(8,128)(2,1)} %copy-done.1, bf16[2,768,384]{2,1,0:T(8,128)(2,1)} %copy-done.2), custom_call_target="tpu_custom_call" | custom-call | flops 900000000 | bytes 5000000 | tf_op jit(solution)/shard_map/pallas_call | solution.py:162
  56.3 0.1 collective-permute-done.5
  56.4 3.4 %collective-permute-start.8 = (f32[64,384]{1,0:T(8,128)S(1)}, f32[64,384]{1,0:T(8,128)S(1)}, u32[]{:S(2)}, u32[]{:S(2)}) collective-permute-start(f32[64,384]{1,0:T(8,128)S(1)} %bitcast.59), channel_id=1, source_target_pairs={{0,4},{4,0},{8,12},{12,8},{1,5},{5,1},{9,13},{13,9},{2,6},{6,2},{1... | collective-permute-start | bytes 294920 | tf_op jit(solution)/shard_map/ppermute | solution.py:180
  59.8 4.1 %all-to-all-start.1 = ((f32[4,64,384]{2,1,0:T(8,128)}), f32[4,64,384]{2,1,0:T(8,128)S(1)}, u32[]{:S(2)}, u32[]{:S(2)}) async-start(f32[4,64,384]{2,1,0:T(8,128)} %shard_map.70), calls=%async_computation.1 | async-start | bytes 786432 | tf_op jit(solution)/shard_map/all_to_all | solution.py:178
  64.0 1.9 %collective-permute-start.9 = (f32[128,384]{1,0:T(8,128)S(1)}, f32[128,384]{1,0:T(8,128)S(1)}, u32[]{:S(2)}, u32[]{:S(2)}) collective-permute-start(f32[128,384]{1,0:T(8,128)S(1)} %bitcast.56), channel_id=1, source_target_pairs={{0,1},{1,0},{2,3},{3,2},{4,5},{5,4},{6,7},{7,6},{8,9},{9,8},{10,11... | collective-permute-start | bytes 589832 | tf_op jit(solution)/shard_map/ppermute | solution.py:182
  66.0 5.3 %all-to-all-done.1 = f32[4,64,384]{2,1,0:T(8,128)S(1)} async-done(((f32[4,64,384]{2,1,0:T(8,128)}), f32[4,64,384]{2,1,0:T(8,128)S(1)}, u32[]{:S(2)}, u32[]{:S(2)}) %all-to-all-start.1) | async-done | bytes 393248 | tf_op jit(solution)/shard_map/all_to_all | solution.py:178
  71.3 15.7 %collective-permute-start.7 = (f32[32,384]{1,0:T(8,128)S(1)}, f32[32,384]{1,0:T(8,128)S(1)}, u32[]{:S(2)}, u32[]{:S(2)}) collective-permute-start(f32[32,384]{1,0:T(8,128)S(1)} %get-tuple-element.16), channel_id=1, source_target_pairs={{0,2},{2,0},{1,3},{3,1},{4,6},{6,4},{5,7},{7,5},{8,10},{10,8},{9,1... | collective-permute-start | bytes 147464 | tf_op jit(solution)/shard_map/ppermute | solution.py:189
  87.1 2.0 %collective-permute-done.7 = f32[32,384]{1,0:T(8,128)S(1)} collective-permute-done((f32[32,384]{1,0:T(8,128)S(1)}, f32[32,384]{1,0:T(8,128)S(1)}, u32[]{:S(2)}, u32[]{:S(2)}) %collective-permute-start.7) | collective-permute-done | bytes 49184 | tf_op jit(solution)/shard_map/ppermute | solution.py:189
  89.1 0.6 fusion.1
  89.7 0.3 fusion.2
  90.1 9.7 %all_to_all.20 = f32[8,32,256]{2,1,0:T(8,128)S(1)} all-to-all(f32[8,32,256]{2,1,0:T(8,128)S(1)} %broadcast_in_dim.29), channel_id=1, replica_groups=mesh['x'=4,'zq'=2,'zm'=2,'z0'=2,'y'=4,'zh'=2,'core'=2] {'x','z0'}, dimensions={0} | all-to-all | bytes 524288 | tf_op jit(solution)/shard_map/all_to_all | solution.py:107
  99.8 19.4 %all_to_all.21 = f32[4,32,256]{2,1,0:T(8,128)S(1)} all-to-all(f32[4,32,256]{2,1,0:T(8,128)S(1)} %broadcast_in_dim.30), channel_id=1, replica_groups=mesh['x'=4,'zq'=2,'zm'=2,'z0'=2,'y'=4,'zh'=2,'core'=2] {'zq','zm'}, dimensions={0} | all-to-all | bytes 262144 | tf_op jit(solution)/shard_map/all_to_all | solution.py:107
  119.2 0.6 bitcast_add_fusion
  (39 shorter events, 0.5 us)
Async XLA Ops:
  0.6 17.1 %collective-permute-start.3 = (f32[16,768]{1,0:T(8,128)}, f32[16,768]{1,0:T(8,128)S(1)}, u32[]{:S(2)}, u32[]{:S(2)}) collective-permute-start(f32[16,768]{1,0:T(8,128)} %bitcast.71), channel_id=1, source_target_pairs={{65,0},{97,1},{67,2},{99,3},{69,4},{101,5},{71,6},{103,7},{73,8},{... | collective-permute-start | bytes 147464 | tf_op jit(solution)/shard_map/ppermute | solution.py:35
  12.4 10.6 %collective-permute-start.2 = (f32[16,768]{1,0:T(8,128)}, f32[16,768]{1,0:T(8,128)S(1)}, u32[]{:S(2)}, u32[]{:S(2)}) collective-permute-start(f32[16,768]{1,0:T(8,128)} %bitcast.72), channel_id=1, source_target_pairs={{64,0},{96,1},{66,2},{98,3},{68,4},{100,5},{70,6},{102,7},{72,8},{... | collective-permute-start | bytes 147464 | tf_op jit(solution)/shard_map/ppermute | solution.py:35
  14.4 8.7 %collective-permute-start.1 = (f32[16,768]{1,0:T(8,128)}, f32[16,768]{1,0:T(8,128)S(1)}, u32[]{:S(2)}, u32[]{:S(2)}) collective-permute-start(f32[16,768]{1,0:T(8,128)} %bitcast.73), channel_id=1, source_target_pairs={{1,0},{33,1},{3,2},{35,3},{5,4},{37,5},{7,6},{39,7},{9,8},{41,9},{... | collective-permute-start | bytes 147464 | tf_op jit(solution)/shard_map/ppermute | solution.py:35
  16.3 6.8 %collective-permute-start = (f32[16,768]{1,0:T(8,128)}, f32[16,768]{1,0:T(8,128)S(1)}, u32[]{:S(2)}, u32[]{:S(2)}) collective-permute-start(f32[16,768]{1,0:T(8,128)} %bitcast.74), channel_id=1, source_target_pairs={{0,0},{32,1},{2,2},{34,3},{4,4},{36,5},{6,6},{38,7},{8,8},{40,9},{... | collective-permute-start | bytes 147464 | tf_op jit(solution)/shard_map/ppermute | solution.py:35
  24.4 6.0 %copy-start = (f32[384,768]{1,0:T(8,128)S(1)}, f32[384,768]{1,0:T(8,128)}, u32[]{:S(2)}) copy-start(f32[384,768]{1,0:T(8,128)} %ancestor_ref.1) | copy-start | bytes 3538948
  24.4 6.0 %copy-start.3 = (s32[3,6]{1,0:T(4,128)S(1)}, s32[3,6]{1,0:T(4,128)}, u32[]{:S(2)}) copy-start(s32[3,6]{1,0:T(4,128)} %pattern_ref.1) | copy-start | bytes 220
  24.4 27.0 %all-to-all-start = ((f32[8,64,768]{2,1,0:T(8,128)}), f32[8,64,768]{2,1,0:T(8,128)}, u32[]{:S(2)}, u32[]{:S(2)}) async-start(f32[8,64,768]{2,1,0:T(8,128)} %broadcast_in_dim.26), calls=%async_computation | async-start | bytes 3145728 | tf_op jit(solution)/shard_map/all_to_all | solution.py:107
  30.4 2.6 %copy-start.5 = (s32[96,2]{0,1:T(2,128)S(1)}, s32[96,2]{0,1:T(2,128)}, u32[]{:S(2)}) copy-start(s32[96,2]{0,1:T(2,128)} %param.7) | copy-start | bytes 2308
  31.0 13.0 %collective-permute-start.4 = (f32[384,768]{1,0:T(8,128)S(1)}, f32[384,768]{1,0:T(8,128)S(1)}, u32[]{:S(2)}, u32[]{:S(2)}) collective-permute-start(f32[384,768]{1,0:T(8,128)S(1)} %shard_map.68.own_ref), channel_id=1, source_target_pairs={{0,1},{1,0},{2,3},{3,2},{4,5},{5,4},{6,7},{7,6},{8,9},{9,8},{10,11... | collective-permute-start | bytes 3538952 | tf_op jit(solution)/shard_map/ppermute | solution.py:133
  34.0 22.3 %collective-permute-start.6 = (f32[32,384]{1,0:T(8,128)S(1)}, f32[32,384]{1,0:T(8,128)S(1)}, u32[]{:S(2)}, u32[]{:S(2)}) collective-permute-start(f32[32,384]{1,0:T(8,128)S(1)} %get-tuple-element.26), channel_id=1, source_target_pairs={{16,0},{17,1},{80,2},{81,3},{144,4},{145,5},{208,6},{209,7},{272,8... | collective-permute-start | bytes 147464 | tf_op jit(solution)/shard_map/ppermute | solution.py:35
  39.8 16.5 %collective-permute-start.5 = (f32[32,384]{1,0:T(8,128)S(1)}, f32[32,384]{1,0:T(8,128)S(1)}, u32[]{:S(2)}, u32[]{:S(2)}) collective-permute-start(f32[32,384]{1,0:T(8,128)S(1)} %get-tuple-element.27), channel_id=1, source_target_pairs={{0,0},{1,1},{64,2},{65,3},{128,4},{129,5},{192,6},{193,7},{256,8},... | collective-permute-start | bytes 147464 | tf_op jit(solution)/shard_map/ppermute | solution.py:35
  44.7 1.0 copy-start.1
  45.8 1.1 copy-start.2
  56.4 7.6 %collective-permute-start.8 = (f32[64,384]{1,0:T(8,128)S(1)}, f32[64,384]{1,0:T(8,128)S(1)}, u32[]{:S(2)}, u32[]{:S(2)}) collective-permute-start(f32[64,384]{1,0:T(8,128)S(1)} %bitcast.59), channel_id=1, source_target_pairs={{0,4},{4,0},{8,12},{12,8},{1,5},{5,1},{9,13},{13,9},{2,6},{6,2},{1... | collective-permute-start | bytes 294920 | tf_op jit(solution)/shard_map/ppermute | solution.py:180
  59.8 11.5 %all-to-all-start.1 = ((f32[4,64,384]{2,1,0:T(8,128)}), f32[4,64,384]{2,1,0:T(8,128)S(1)}, u32[]{:S(2)}, u32[]{:S(2)}) async-start(f32[4,64,384]{2,1,0:T(8,128)} %shard_map.70), calls=%async_computation.1 | async-start | bytes 786432 | tf_op jit(solution)/shard_map/all_to_all | solution.py:178
  64.0 23.1 %collective-permute-start.9 = (f32[128,384]{1,0:T(8,128)S(1)}, f32[128,384]{1,0:T(8,128)S(1)}, u32[]{:S(2)}, u32[]{:S(2)}) collective-permute-start(f32[128,384]{1,0:T(8,128)S(1)} %bitcast.56), channel_id=1, source_target_pairs={{0,1},{1,0},{2,3},{3,2},{4,5},{5,4},{6,7},{7,6},{8,9},{9,8},{10,11... | collective-permute-start | bytes 589832 | tf_op jit(solution)/shard_map/ppermute | solution.py:182
  71.3 17.8 %collective-permute-start.7 = (f32[32,384]{1,0:T(8,128)S(1)}, f32[32,384]{1,0:T(8,128)S(1)}, u32[]{:S(2)}, u32[]{:S(2)}) collective-permute-start(f32[32,384]{1,0:T(8,128)S(1)} %get-tuple-element.16), channel_id=1, source_target_pairs={{0,2},{2,0},{1,3},{3,1},{4,6},{6,4},{5,7},{7,5},{8,10},{10,8},{9,1... | collective-permute-start | bytes 147464 | tf_op jit(solution)/shard_map/ppermute | solution.py:189
  89.1 30.1 %copy-start.4 = (f32[256,32]{0,1:T(8,128)S(1)}, f32[256,32]{0,1:T(8,128)}, u32[]{:S(2)}) copy-start(f32[256,32]{0,1:T(8,128)} %param.9) | copy-start | bytes 98308

commit v7 on v6

--- a/solution.py
+++ b/solution.py
@@ -59,18 +59,24 @@
 
 
 def block_product(
-    turn_ref, full_hbm, keep_ref, high_hbm, low_hbm, out_ref, full_ref, high_ref, low_ref, sems
+    turn_ref, full_hbm, keep_ref, high_ref, low_hbm, out_ref, full_ref, low_ref, sems
 ):
     turn = turn_ref[0]
-    fetched = [pltpu.make_async_copy(full_hbm, full_ref, sems.at[0])]
+
+    def fetch_rows(j, zq):
+        here = pl.ds((2 * zq + j) * 16, 16)
+        return pltpu.make_async_copy(full_hbm.at[:, here], full_ref.at[:, here], sems.at[2 * j + zq])
+
+    row_copies = [[fetch_rows(j, zq) for zq in range(2)] for j in range(2)]
+    low_copies = [
+        pltpu.make_async_copy(low_hbm.at[turn ^ j], low_ref.at[j], sems.at[4 + j]) for j in range(2)
+    ]
+    for copy in (*row_copies[0], *row_copies[1], *low_copies):
+        copy.start()
+    total, highs = 0.0, []
     for j in range(2):
-        for n, (hbm, ref) in enumerate(((high_hbm, high_ref), (low_hbm, low_ref))):
-            fetched.append(pltpu.make_async_copy(hbm.at[turn ^ j], ref.at[j], sems.at[1 + 2 * j + n]))
-    for copy in fetched:
-        copy.start()
-    fetched[0].wait()
-    total = 0.0
-    for j in range(2):
+        for copy in row_copies[j]:
+            copy.wait()
         lines = []
         for x in range(4):
             for zq in range(2):
@@ -78,10 +84,12 @@
                     block = full_ref[2 * x + z0, pl.ds((2 * zq + j) * 16, 16), :]
                     lines.append(block * keep_ref[pl.ds(2 * j + x // 2, 1), :])
         high, low = parts_of(jnp.concatenate(lines, axis=0))
-        fetched[1 + 2 * j].wait()
-        fetched[2 + 2 * j].wait()
-        for left, right_ref in ((high, high_ref), (high, low_ref), (low, high_ref)):
-            total += jnp.dot(left, right_ref[j], preferred_element_type=jnp.float32)
+        highs.append(high)
+        for left in (high, low):
+            total += jnp.dot(left, high_ref[turn ^ j], preferred_element_type=jnp.float32)
+    for j in range(2):
+        low_copies[j].wait()
+        total += jnp.dot(highs[j], low_ref[j], preferred_element_type=jnp.float32)
     out_ref[...] = total.reshape(out_ref.shape)
 
 
@@ -162,19 +170,17 @@
     pieces = kernel_call(
         block_product,
         jax.ShapeDtypeStruct((4, 4 * share, rows), jnp.float32),
-        [IN_SMEM, IN_HBM, IN_VMEM, IN_HBM, IN_HBM],
+        [IN_SMEM, IN_HBM, IN_VMEM, IN_VMEM, IN_HBM],
         IN_VMEM,
-        62000000,
+        54000000,
         900 * 10**6,
         5 * 10**6,
         [
             pltpu.VMEM((8, 4 * share, cols), jnp.float32),
             pltpu.VMEM((2, cols, rows), jnp.bfloat16),
-            pltpu.VMEM((2, cols, rows), jnp.bfloat16),
-            pltpu.SemaphoreType.DMA((5,)),
+            pltpu.SemaphoreType.DMA((6,)),
         ],
     )((zm ^ core).reshape(1), full, keep_cols, high, low)
-    pieces, *near = lax.optimization_barrier((pieces, *near))
     pieces = lax.all_to_all(pieces, "y", 0, 0, tiled=True).reshape(4, 2, 2 * share, rows)
     near = jnp.stack(swapped(z0, near[0], near[1]), axis=1).reshape(4 * share, rows)
     far = lax.ppermute(near, "y", [(i, i ^ 1) for i in range(4)])
@@ -192,7 +198,10 @@
     kept, inverse = lax.optimization_barrier((kept, -kept))
     term = product(kept, normed)
     term = copies(term, 8, ("x", "z0")).reshape(8, 2 * share, W).sum(0)
-    term = copies(term, 4, ("zq", "zm")).reshape(4, 2 * share, W).sum(0)
+    far, farther, close = (
+        lax.ppermute(term, ("zq", "zm"), [(i, i ^ k) for i in range(4)]) for k in (2, 3, 1)
+    )
+    term = (term + close) + (far + farther)
     return inverse.T, diag_inv + term.T
 
 

time: 121 us -> 133 us (1.099)
  waiting for transfers between devices: 17.2 us -> 41.3 us
  blocking collectives: 29.1 us -> 9.52 us
  starting transfers between devices: 60.2 us -> 68.9 us
  other arithmetic: 1.48 us -> 3.17 us
  local copies, waits for them, and re-layouts: 4.41 us -> 2.72 us
    all_to_all x2 -> x1, blocking collectives: 29.1 us -> 9.52 us  [copies(): lax.all_to_all(jnp.broadcast_to(block[None], (count,) + block.shape), axe...]
    ppermute x0 -> x3, starting transfers between devices: none -> 18.1 us  [body(): lax.ppermute(term, ('zq', 'zm'), [(i, i ^ k) for i in range(4)])]
    ppermute x6, waiting for transfers between devices: 5.41 us -> 18.2 us  [send(): return lax.ppermute(values, ROW + COL, pairs_to(source_of))]
    ppermute x1, starting transfers between devices: 15.7 us -> 8.43 us  [body(): arrived = lax.ppermute(theirs, 'zh', [(0, 1), (1, 0)])]
    ppermute x1, waiting for transfers between devices: 0.01 us -> 4.69 us  [body(): far = lax.ppermute(near, 'y', [(i, i ^ 1) for i in range(4)])]
    all_to_all x1, waiting for transfers between devices: 4.51 us -> 0.01 us  [copies(): lax.all_to_all(jnp.broadcast_to(block[None], (count,) + block.shape), axe...]
    ppermute x1, waiting for transfers between devices: 1.97 us -> 6.32 us  [body(): arrived = lax.ppermute(theirs, 'zh', [(0, 1), (1, 0)])]
    ppermute x0 -> x3, waiting for transfers between devices: none -> 4.22 us  [body(): lax.ppermute(term, ('zq', 'zm'), [(i, i ^ k) for i in range(4)])]
  transfers between devices with their start and end apart: 12 -> 15, of which waited for: 5 -> 7; matrix products, arithmetic and copies ran while one was open for 1% -> 2% of each run, Pallas kernels for 5% -> 4%
where the time goes in v7:
time: 133 us; the launch traced here: 132 us
  starting transfers between devices  68.9 us (52%)
  waiting for transfers between devices  41.3 us (31%)
  blocking collectives  9.52 us (7%)
  Pallas kernels  5.1 us (4%)
  other arithmetic  3.17 us (2%)
  local copies, waits for them, and re-layouts  2.72 us (2%)
    ppermute x6, starting transfers between devices, send(): return lax.ppermute(values, ROW + COL, pairs_to(source_of))  27.2 us
    ppermute x6, waiting for transfers between devices, send(): return lax.ppermute(values, ROW + COL, pairs_to(source_of))  18.2 us
    ppermute x3, starting transfers between devices, body(): lax.ppermute(term, ('zq', 'zm'), [(i, i ^ k) for i in range(4)])  18.1 us
    all_to_all x1, blocking collectives, copies(): lax.all_to_all(jnp.broadcast_to(block[None], (count,) + block.shape), axe...  9.52 us
    ppermute x1, starting transfers between devices, body(): arrived = lax.ppermute(theirs, 'zh', [(0, 1), (1, 0)])  8.43 us
    all_to_all x1, waiting for transfers between devices, body(): lax.all_to_all(pieces, 'y', 0, 0, tiled=True).reshape(4, 2, 2 * share, rows)  7.85 us
    ppermute x1, waiting for transfers between devices, body(): arrived = lax.ppermute(theirs, 'zh', [(0, 1), (1, 0)])  6.32 us
    all_to_all x1, starting transfers between devices, copies(): lax.all_to_all(jnp.broadcast_to(block[None], (count,) + block.shape), axe...  5.97 us
  transfers between devices with their start and end apart: 15, of which 7 were waited for; matrix products, arithmetic and copies ran while one was open for 2% of the time, Pallas kernels for 4%

profile of v7, /device:TPU:6, one launch (start us, length us, event | category | flops | bytes accessed | tf_op | source)
XLA Modules:
  0.0 131.9 jit_solution(8288716307826326058)
XLA Ops:
  0.6 11.8 %collective-permute-start.3 = (f32[16,768]{1,0:T(8,128)}, f32[16,768]{1,0:T(8,128)S(1)}, u32[]{:S(2)}, u32[]{:S(2)}) collective-permute-start(f32[16,768]{1,0:T(8,128)} %bitcast.62), channel_id=1, source_target_pairs={{65,0},{97,1},{67,2},{99,3},{69,4},{101,5},{71,6},{103,7},{73,8},{... | collective-permute-start | bytes 147464 | tf_op jit(solution)/shard_map/ppermute | solution.py:35
  12.4 1.9 %collective-permute-start.2 = (f32[16,768]{1,0:T(8,128)}, f32[16,768]{1,0:T(8,128)S(1)}, u32[]{:S(2)}, u32[]{:S(2)}) collective-permute-start(f32[16,768]{1,0:T(8,128)} %bitcast.63), channel_id=1, source_target_pairs={{64,0},{96,1},{66,2},{98,3},{68,4},{100,5},{70,6},{102,7},{72,8},{... | collective-permute-start | bytes 147464 | tf_op jit(solution)/shard_map/ppermute | solution.py:35
  14.4 1.9 %collective-permute-start.1 = (f32[16,768]{1,0:T(8,128)}, f32[16,768]{1,0:T(8,128)S(1)}, u32[]{:S(2)}, u32[]{:S(2)}) collective-permute-start(f32[16,768]{1,0:T(8,128)} %bitcast.64), channel_id=1, source_target_pairs={{1,0},{33,1},{3,2},{35,3},{5,4},{37,5},{7,6},{39,7},{9,8},{41,9},{... | collective-permute-start | bytes 147464 | tf_op jit(solution)/shard_map/ppermute | solution.py:35
  16.3 1.5 %collective-permute-start = (f32[16,768]{1,0:T(8,128)}, f32[16,768]{1,0:T(8,128)S(1)}, u32[]{:S(2)}, u32[]{:S(2)}) collective-permute-start(f32[16,768]{1,0:T(8,128)} %bitcast.65), channel_id=1, source_target_pairs={{0,0},{32,1},{2,2},{34,3},{4,4},{36,5},{6,6},{38,7},{8,8},{40,9},{... | collective-permute-start | bytes 147464 | tf_op jit(solution)/shard_map/ppermute | solution.py:35
  17.8 5.3 %collective-permute-done.2 = f32[16,768]{1,0:T(8,128)S(1)} collective-permute-done((f32[16,768]{1,0:T(8,128)}, f32[16,768]{1,0:T(8,128)S(1)}, u32[]{:S(2)}, u32[]{:S(2)}) %collective-permute-start.2) | collective-permute-done | bytes 49184 | tf_op jit(solution)/shard_map/ppermute | solution.py:35
  23.1 1.3 broadcast_in_dim.20
  24.4 6.0 %all-to-all-start = ((f32[8,64,768]{2,1,0:T(8,128)}), f32[8,64,768]{2,1,0:T(8,128)}, u32[]{:S(2)}, u32[]{:S(2)}) async-start(f32[8,64,768]{2,1,0:T(8,128)} %broadcast_in_dim.20), calls=%async_computation | async-start | bytes 3145728 | tf_op jit(solution)/shard_map/all_to_all | solution.py:115
  30.4 0.6 shard_map.68.own_ref
  31.0 1.9 %collective-permute-start.4 = (f32[384,768]{1,0:T(8,128)S(1)}, f32[384,768]{1,0:T(8,128)S(1)}, u32[]{:S(2)}, u32[]{:S(2)}) collective-permute-start(f32[384,768]{1,0:T(8,128)S(1)} %shard_map.68.own_ref), channel_id=1, source_target_pairs={{0,1},{1,0},{2,3},{3,2},{4,5},{5,4},{6,7},{7,6},{8,9},{9,8},{10,11... | collective-permute-start | bytes 3538952 | tf_op jit(solution)/shard_map/ppermute | solution.py:141
  33.3 4.6 %collective-permute-start.6 = (f32[32,384]{1,0:T(8,128)S(1)}, f32[32,384]{1,0:T(8,128)S(1)}, u32[]{:S(2)}, u32[]{:S(2)}) collective-permute-start(f32[32,384]{1,0:T(8,128)S(1)} %get-tuple-element.20), channel_id=1, source_target_pairs={{0,0},{1,1},{64,2},{65,3},{128,4},{129,5},{192,6},{193,7},{256,8},... | collective-permute-start | bytes 147464 | tf_op jit(solution)/shard_map/ppermute | solution.py:35
  37.9 5.5 %collective-permute-start.7 = (f32[32,384]{1,0:T(8,128)S(1)}, f32[32,384]{1,0:T(8,128)S(1)}, u32[]{:S(2)}, u32[]{:S(2)}) collective-permute-start(f32[32,384]{1,0:T(8,128)S(1)} %get-tuple-element.21), channel_id=1, source_target_pairs={{16,0},{17,1},{80,2},{81,3},{144,4},{145,5},{208,6},{209,7},{272,8... | collective-permute-start | bytes 147464 | tf_op jit(solution)/shard_map/ppermute | solution.py:35
  43.5 12.9 %collective-permute-done.6 = f32[32,384]{1,0:T(8,128)S(1)} collective-permute-done((f32[32,384]{1,0:T(8,128)S(1)}, f32[32,384]{1,0:T(8,128)S(1)}, u32[]{:S(2)}, u32[]{:S(2)}) %collective-permute-start.6) | collective-permute-done | bytes 49184 | tf_op jit(solution)/shard_map/ppermute | solution.py:35
  56.4 1.9 %collective-permute-start.8 = (f32[64,384]{1,0:T(8,128)S(1)}, f32[64,384]{1,0:T(8,128)S(1)}, u32[]{:S(2)}, u32[]{:S(2)}) collective-permute-start(f32[64,384]{1,0:T(8,128)S(1)} %bitcast.52), channel_id=1, source_target_pairs={{0,4},{4,0},{8,12},{12,8},{1,5},{5,1},{9,13},{13,9},{2,6},{6,2},{1... | collective-permute-start | bytes 294920 | tf_op jit(solution)/shard_map/ppermute | solution.py:186
  58.3 4.7 %collective-permute-done.8 = f32[64,384]{1,0:T(8,128)S(1)} collective-permute-done((f32[64,384]{1,0:T(8,128)S(1)}, f32[64,384]{1,0:T(8,128)S(1)}, u32[]{:S(2)}, u32[]{:S(2)}) %collective-permute-start.8) | collective-permute-done | bytes 98336 | tf_op jit(solution)/shard_map/ppermute | solution.py:186
  63.1 0.7 pad_maximum_fusion.2
  63.8 1.9 %collective-permute-start.9 = (f32[128,384]{1,0:T(8,128)}, f32[128,384]{1,0:T(8,128)}, u32[]{:S(2)}, u32[]{:S(2)}) collective-permute-start(f32[128,384]{1,0:T(8,128)} %bitcast.23), channel_id=1, source_target_pairs={{0,1},{1,0},{2,3},{3,2},{4,5},{5,4},{6,7},{7,6},{8,9},{9,8},{10,11... | collective-permute-start | bytes 589832 | tf_op jit(solution)/shard_map/ppermute | solution.py:188
  65.7 0.7 shard_map.69
  66.4 1.0 copy-done.1
  67.4 3.8 %shard_map.70 = f32[4,64,384]{2,1,0:T(8,128)} custom-call(s32[1]{0:T(128)} %bitcast.turn_ref, f32[8,64,768]{2,1,0:T(8,128)} %all-to-all-done.full_hbm, f32[4,768]{1,0:T(4,128)S(1)} %bitcast.47, bf16[2,768,384]{2,1,0:T(8,128)(2,1)S(1)} %get-tuple-element.6.high_ref, bf16[2,768,384]{2,1,0:T(8,128)(2,1)} %copy-done.1), custom_call_target="tpu_custom_call" | custom-call | flops 900000000 | bytes 5000000 | tf_op jit(solution)/shard_map/pallas_call | solution.py:170
  71.2 3.5 %all-to-all-start.1 = ((f32[4,64,384]{2,1,0:T(8,128)}), f32[4,64,384]{2,1,0:T(8,128)S(1)}, u32[]{:S(2)}, u32[]{:S(2)}) async-start(f32[4,64,384]{2,1,0:T(8,128)} %shard_map.70), calls=%async_computation.1 | async-start | bytes 786432 | tf_op jit(solution)/shard_map/all_to_all | solution.py:184
  74.7 1.1 broadcast_select_fusion.1
  75.8 7.9 %all-to-all-done.1 = f32[4,64,384]{2,1,0:T(8,128)S(1)} async-done(((f32[4,64,384]{2,1,0:T(8,128)}), f32[4,64,384]{2,1,0:T(8,128)S(1)}, u32[]{:S(2)}, u32[]{:S(2)}) %all-to-all-start.1) | async-done | bytes 393248 | tf_op jit(solution)/shard_map/all_to_all | solution.py:184
  83.7 8.4 %collective-permute-start.5 = (f32[32,384]{1,0:T(8,128)S(1)}, f32[32,384]{1,0:T(8,128)S(1)}, u32[]{:S(2)}, u32[]{:S(2)}) collective-permute-start(f32[32,384]{1,0:T(8,128)S(1)} %get-tuple-element.10), channel_id=1, source_target_pairs={{0,2},{2,0},{1,3},{3,1},{4,6},{6,4},{5,7},{7,5},{8,10},{10,8},{9,1... | collective-permute-start | bytes 147464 | tf_op jit(solution)/shard_map/ppermute | solution.py:195
  92.1 6.3 %collective-permute-done.5 = f32[32,384]{1,0:T(8,128)S(1)} collective-permute-done((f32[32,384]{1,0:T(8,128)S(1)}, f32[32,384]{1,0:T(8,128)S(1)}, u32[]{:S(2)}, u32[]{:S(2)}) %collective-permute-start.5) | collective-permute-done | bytes 49184 | tf_op jit(solution)/shard_map/ppermute | solution.py:195
  98.5 0.6 fusion.1
  99.4 9.5 %all_to_all.15 = f32[8,32,256]{2,1,0:T(8,128)S(1)} all-to-all(f32[8,32,256]{2,1,0:T(8,128)S(1)} %broadcast_in_dim.23), channel_id=1, replica_groups=mesh['x'=4,'zq'=2,'zm'=2,'z0'=2,'y'=4,'zh'=2,'core'=2] {'x','z0'}, dimensions={0} | all-to-all | bytes 524288 | tf_op jit(solution)/shard_map/all_to_all | solution.py:115
  108.9 9.9 %collective-permute-start.12 = (f32[32,256]{1,0:T(8,128)S(1)}, f32[32,256]{1,0:T(8,128)S(1)}, u32[]{:S(2)}, u32[]{:S(2)}) collective-permute-start(f32[32,256]{1,0:T(8,128)S(1)} %reduce_sum.29), channel_id=1, source_target_pairs={{0,96},{32,64},{64,32},{96,0},{1,97},{33,65},{65,33},{97,1},{2,98}... | collective-permute-start | bytes 98312 | tf_op jit(solution)/shard_map/ppermute | solution.py:202
  118.9 5.7 %collective-permute-start.11 = (f32[32,256]{1,0:T(8,128)S(1)}, f32[32,256]{1,0:T(8,128)S(1)}, u32[]{:S(2)}, u32[]{:S(2)}) collective-permute-start(f32[32,256]{1,0:T(8,128)S(1)} %reduce_sum.29), channel_id=1, source_target_pairs={{0,64},{32,96},{64,0},{96,32},{1,65},{33,97},{65,1},{97,33},{2,66}... | collective-permute-start | bytes 98312 | tf_op jit(solution)/shard_map/ppermute | solution.py:202
  124.6 2.5 %collective-permute-start.10 = (f32[32,256]{1,0:T(8,128)S(1)}, f32[32,256]{1,0:T(8,128)S(1)}, u32[]{:S(2)}, u32[]{:S(2)}) collective-permute-start(f32[32,256]{1,0:T(8,128)S(1)} %reduce_sum.29), channel_id=1, source_target_pairs={{0,32},{32,0},{64,96},{96,64},{1,33},{33,1},{65,97},{97,65},{2,34}... | collective-permute-start | bytes 98312 | tf_op jit(solution)/shard_map/ppermute | solution.py:202
  127.1 1.5 %collective-permute-done.11 = f32[32,256]{1,0:T(8,128)S(1)} collective-permute-done((f32[32,256]{1,0:T(8,128)S(1)}, f32[32,256]{1,0:T(8,128)S(1)}, u32[]{:S(2)}, u32[]{:S(2)}) %collective-permute-start.11) | collective-permute-done | bytes 32800 | tf_op jit(solution)/shard_map/ppermute | solution.py:202
  128.6 2.7 %collective-permute-done.10 = f32[32,256]{1,0:T(8,128)S(1)} collective-permute-done((f32[32,256]{1,0:T(8,128)S(1)}, f32[32,256]{1,0:T(8,128)S(1)}, u32[]{:S(2)}, u32[]{:S(2)}) %collective-permute-start.10) | collective-permute-done | bytes 32800 | tf_op jit(solution)/shard_map/ppermute | solution.py:202
  131.3 0.6 bitcast_add_fusion
  (40 shorter events, 0.9 us)
Async XLA Ops:
  0.6 17.1 %collective-permute-start.3 = (f32[16,768]{1,0:T(8,128)}, f32[16,768]{1,0:T(8,128)S(1)}, u32[]{:S(2)}, u32[]{:S(2)}) collective-permute-start(f32[16,768]{1,0:T(8,128)} %bitcast.62), channel_id=1, source_target_pairs={{65,0},{97,1},{67,2},{99,3},{69,4},{101,5},{71,6},{103,7},{73,8},{... | collective-permute-start | bytes 147464 | tf_op jit(solution)/shard_map/ppermute | solution.py:35
  12.4 10.6 %collective-permute-start.2 = (f32[16,768]{1,0:T(8,128)}, f32[16,768]{1,0:T(8,128)S(1)}, u32[]{:S(2)}, u32[]{:S(2)}) collective-permute-start(f32[16,768]{1,0:T(8,128)} %bitcast.63), channel_id=1, source_target_pairs={{64,0},{96,1},{66,2},{98,3},{68,4},{100,5},{70,6},{102,7},{72,8},{... | collective-permute-start | bytes 147464 | tf_op jit(solution)/shard_map/ppermute | solution.py:35
  14.4 8.7 %collective-permute-start.1 = (f32[16,768]{1,0:T(8,128)}, f32[16,768]{1,0:T(8,128)S(1)}, u32[]{:S(2)}, u32[]{:S(2)}) collective-permute-start(f32[16,768]{1,0:T(8,128)} %bitcast.64), channel_id=1, source_target_pairs={{1,0},{33,1},{3,2},{35,3},{5,4},{37,5},{7,6},{39,7},{9,8},{41,9},{... | collective-permute-start | bytes 147464 | tf_op jit(solution)/shard_map/ppermute | solution.py:35
  16.3 6.8 %collective-permute-start = (f32[16,768]{1,0:T(8,128)}, f32[16,768]{1,0:T(8,128)S(1)}, u32[]{:S(2)}, u32[]{:S(2)}) collective-permute-start(f32[16,768]{1,0:T(8,128)} %bitcast.65), channel_id=1, source_target_pairs={{0,0},{32,1},{2,2},{34,3},{4,4},{36,5},{6,6},{38,7},{8,8},{40,9},{... | collective-permute-start | bytes 147464 | tf_op jit(solution)/shard_map/ppermute | solution.py:35
  24.4 6.0 %copy-start = (f32[384,768]{1,0:T(8,128)S(1)}, f32[384,768]{1,0:T(8,128)}, u32[]{:S(2)}) copy-start(f32[384,768]{1,0:T(8,128)} %ancestor_ref.1) | copy-start | bytes 3538948
  24.4 6.0 %copy-start.2 = (s32[3,6]{1,0:T(4,128)S(1)}, s32[3,6]{1,0:T(4,128)}, u32[]{:S(2)}) copy-start(s32[3,6]{1,0:T(4,128)} %pattern_ref.1) | copy-start | bytes 220
  24.4 43.0 %all-to-all-start = ((f32[8,64,768]{2,1,0:T(8,128)}), f32[8,64,768]{2,1,0:T(8,128)}, u32[]{:S(2)}, u32[]{:S(2)}) async-start(f32[8,64,768]{2,1,0:T(8,128)} %broadcast_in_dim.20), calls=%async_computation | async-start | bytes 3145728 | tf_op jit(solution)/shard_map/all_to_all | solution.py:115
  30.3 2.6 %copy-start.4 = (s32[96,2]{0,1:T(2,128)S(1)}, s32[96,2]{0,1:T(2,128)}, u32[]{:S(2)}) copy-start(s32[96,2]{0,1:T(2,128)} %param.7) | copy-start | bytes 2308
  31.0 34.7 %collective-permute-start.4 = (f32[384,768]{1,0:T(8,128)S(1)}, f32[384,768]{1,0:T(8,128)S(1)}, u32[]{:S(2)}, u32[]{:S(2)}) collective-permute-start(f32[384,768]{1,0:T(8,128)S(1)} %shard_map.68.own_ref), channel_id=1, source_target_pairs={{0,1},{1,0},{2,3},{3,2},{4,5},{5,4},{6,7},{7,6},{8,9},{9,8},{10,11... | collective-permute-start | bytes 3538952 | tf_op jit(solution)/shard_map/ppermute | solution.py:141
  33.3 23.0 %collective-permute-start.6 = (f32[32,384]{1,0:T(8,128)S(1)}, f32[32,384]{1,0:T(8,128)S(1)}, u32[]{:S(2)}, u32[]{:S(2)}) collective-permute-start(f32[32,384]{1,0:T(8,128)S(1)} %get-tuple-element.20), channel_id=1, source_target_pairs={{0,0},{1,1},{64,2},{65,3},{128,4},{129,5},{192,6},{193,7},{256,8},... | collective-permute-start | bytes 147464 | tf_op jit(solution)/shard_map/ppermute | solution.py:35
  37.9 18.4 %collective-permute-start.7 = (f32[32,384]{1,0:T(8,128)S(1)}, f32[32,384]{1,0:T(8,128)S(1)}, u32[]{:S(2)}, u32[]{:S(2)}) collective-permute-start(f32[32,384]{1,0:T(8,128)S(1)} %get-tuple-element.21), channel_id=1, source_target_pairs={{16,0},{17,1},{80,2},{81,3},{144,4},{145,5},{208,6},{209,7},{272,8... | collective-permute-start | bytes 147464 | tf_op jit(solution)/shard_map/ppermute | solution.py:35
  56.4 6.7 %collective-permute-start.8 = (f32[64,384]{1,0:T(8,128)S(1)}, f32[64,384]{1,0:T(8,128)S(1)}, u32[]{:S(2)}, u32[]{:S(2)}) collective-permute-start(f32[64,384]{1,0:T(8,128)S(1)} %bitcast.52), channel_id=1, source_target_pairs={{0,4},{4,0},{8,12},{12,8},{1,5},{5,1},{9,13},{13,9},{2,6},{6,2},{1... | collective-permute-start | bytes 294920 | tf_op jit(solution)/shard_map/ppermute | solution.py:186
  63.8 11.0 %collective-permute-start.9 = (f32[128,384]{1,0:T(8,128)}, f32[128,384]{1,0:T(8,128)}, u32[]{:S(2)}, u32[]{:S(2)}) collective-permute-start(f32[128,384]{1,0:T(8,128)} %bitcast.23), channel_id=1, source_target_pairs={{0,1},{1,0},{2,3},{3,2},{4,5},{5,4},{6,7},{7,6},{8,9},{9,8},{10,11... | collective-permute-start | bytes 589832 | tf_op jit(solution)/shard_map/ppermute | solution.py:188
  66.4 1.0 copy-start.1
  71.2 12.5 %all-to-all-start.1 = ((f32[4,64,384]{2,1,0:T(8,128)}), f32[4,64,384]{2,1,0:T(8,128)S(1)}, u32[]{:S(2)}, u32[]{:S(2)}) async-start(f32[4,64,384]{2,1,0:T(8,128)} %shard_map.70), calls=%async_computation.1 | async-start | bytes 786432 | tf_op jit(solution)/shard_map/all_to_all | solution.py:184
  83.7 14.8 %collective-permute-start.5 = (f32[32,384]{1,0:T(8,128)S(1)}, f32[32,384]{1,0:T(8,128)S(1)}, u32[]{:S(2)}, u32[]{:S(2)}) collective-permute-start(f32[32,384]{1,0:T(8,128)S(1)} %get-tuple-element.10), channel_id=1, source_target_pairs={{0,2},{2,0},{1,3},{3,1},{4,6},{6,4},{5,7},{7,5},{8,10},{10,8},{9,1... | collective-permute-start | bytes 147464 | tf_op jit(solution)/shard_map/ppermute | solution.py:195
  92.1 39.2 %copy-start.3 = (f32[256,32]{0,1:T(8,128)S(1)}, f32[256,32]{0,1:T(8,128)}, u32[]{:S(2)}) copy-start(f32[256,32]{0,1:T(8,128)} %param.9) | copy-start | bytes 98308
  108.9 18.1 %collective-permute-start.12 = (f32[32,256]{1,0:T(8,128)S(1)}, f32[32,256]{1,0:T(8,128)S(1)}, u32[]{:S(2)}, u32[]{:S(2)}) collective-permute-start(f32[32,256]{1,0:T(8,128)S(1)} %reduce_sum.29), channel_id=1, source_target_pairs={{0,96},{32,64},{64,32},{96,0},{1,97},{33,65},{65,33},{97,1},{2,98}... | collective-permute-start | bytes 98312 | tf_op jit(solution)/shard_map/ppermute | solution.py:202
  118.9 9.7 %collective-permute-start.11 = (f32[32,256]{1,0:T(8,128)S(1)}, f32[32,256]{1,0:T(8,128)S(1)}, u32[]{:S(2)}, u32[]{:S(2)}) collective-permute-start(f32[32,256]{1,0:T(8,128)S(1)} %reduce_sum.29), channel_id=1, source_target_pairs={{0,64},{32,96},{64,0},{96,32},{1,65},{33,97},{65,1},{97,33},{2,66}... | collective-permute-start | bytes 98312 | tf_op jit(solution)/shard_map/ppermute | solution.py:202
  124.6 6.7 %collective-permute-start.10 = (f32[32,256]{1,0:T(8,128)S(1)}, f32[32,256]{1,0:T(8,128)S(1)}, u32[]{:S(2)}, u32[]{:S(2)}) collective-permute-start(f32[32,256]{1,0:T(8,128)S(1)} %reduce_sum.29), channel_id=1, source_target_pairs={{0,32},{32,0},{64,96},{96,64},{1,33},{33,1},{65,97},{97,65},{2,34}... | collective-permute-start | bytes 98312 | tf_op jit(solution)/shard_map/ppermute | solution.py:202
